TPU v7x, 256 devices: a whole 4x4x8 slice. The times are simulated.
256 devices in a mesh: cls: 32 (over x, y, core), prt: 8 (over z).
Axes of the slice: x: 4, y: 4, z: 8, core: 2. Of those that a mesh axis runs over, the one named last changes fastest.
Arguments:
- particles: bfloat16 [4096, 128, 512], P(('cls', 'prt')), may hold values from -20100 to 20100
- references: bfloat16 [512, 128, 512], P('cls'), may hold values from -6 to 6
- owner_groups: int32 [4096, 4], P(('cls', 'prt')), may hold values from 0 to 31, all different within a row; in each aligned block of 16 rows (0 to 15, 16 to 31, ...) at most 4 rows name the same one
- class_order: int32 [4096, 4, 16], P(('cls', 'prt')), may hold values from 0 to 15, each once within a row
Outputs:
- class_sums: float32 [512, 128, 512], P('cls', 'prt')
- class_weights: float32 [512], P('cls')
- log_norm: float32 [4096], P(('cls', 'prt'))
Inputs may be any that keep to these rules, and one draw needn't show every extreme that they name: `owner_groups`: each row names 4 different groups. Among the 16 particles of one device, no group is named by more than 4 rows, a bound that some block reaches. `class_order`: each row along the last dimension is a permutation.
All inputs are finite; a program needn't handle non-finite values.
Results may differ from a plain program's by a relative error of at most 0.0029.
Values may be sent and summed in bfloat16 or wider, within the bound.
A program may use at most 128 MiB of HBM per device.

v0:
```python
import math

import jax
import jax.numpy as jnp
from jax import lax
from jax.sharding import PartitionSpec as P

CYCLES = 128
HARM = 256
ROTS = 36
OWN_TOP = 4
CAND_OWN = 4


lowest = -1e30


def cut_along(x, dim, devices):
    shape = x.shape
    pieces = x.reshape(*shape[:dim], devices, shape[dim] // devices, *shape[dim + 1 :])
    return jnp.moveaxis(pieces, dim, 0)


def edges_of(length, count):
    turn = length // count
    if turn >= 8:
        turn -= turn % 8
    return [turn * k for k in range(1, count)]


def joined_along(pieces, dim):
    pieces = jnp.moveaxis(pieces, 0, dim)
    shape = pieces.shape
    return pieces.reshape(*shape[:dim], shape[dim] * shape[dim + 1], *shape[dim + 2 :])


def several_exchanges(x, axis, pieces, split_dim, concat_dim):
    blocks = cut_along(x, split_dim, lax.axis_size(axis))
    widest = max(range(1, max(2, blocks.ndim - 1)), key=lambda d: blocks.shape[d])
    outs = []
    for slab in jnp.split(blocks, edges_of(blocks.shape[widest], pieces), axis=widest):
        if slab.size:
            outs.append(lax.all_to_all(slab, axis, split_axis=0, concat_axis=0, tiled=True))
    return joined_along(jnp.concatenate(outs, axis=widest), concat_dim)


def sent_to_all(x, axis):
    devices = lax.axis_size(axis)
    return lax.all_to_all(jnp.broadcast_to(x[None], (devices, *x.shape)), axis, 0, 0, tiled=True)


def collect(x, axis, dim):
    pieces = sent_to_all(x, axis)
    return joined_along(pieces, dim)


def side_by_side(arrays, axis, dim, along):
    both = jnp.concatenate(arrays, axis=along)
    filled, at, outs = (collect(both, axis, dim), 0, [])
    for a in arrays:
        outs.append(lax.slice_in_dim(filled, at, at + a.shape[along], axis=along))
        at += a.shape[along]
    return tuple(outs)


def taken_together(x, axis):
    everything = sent_to_all(x, axis)
    return jnp.sum(everything, axis=0)


def spectral_tables():
    harmonic = jnp.arange(HARM, dtype=jnp.float32)
    angles = 2.0 * math.pi * jnp.arange(ROTS, dtype=jnp.float32) / ROTS
    phase = harmonic[:, None] * angles[None, :]
    forward = jnp.concatenate([jnp.cos(phase), jnp.sin(phase)], 0)
    backward = jnp.concatenate([jnp.cos(phase), -jnp.sin(phase)], 0).T
    return (forward, backward)


def class_accumulate(lanes, mixed):
    l_re = lanes[..., :HARM]
    l_im = lanes[..., HARM:]
    y_re = mixed[..., :HARM]
    y_im = mixed[..., HARM:]
    s_re = jnp.einsum("lrm,lcm->crm", l_re, y_re, preferred_element_type=jnp.float32) - jnp.einsum(
        "lrm,lcm->crm", l_im, y_im, preferred_element_type=jnp.float32
    )
    s_im = jnp.einsum("lrm,lcm->crm", l_re, y_im, preferred_element_type=jnp.float32) + jnp.einsum(
        "lrm,lcm->crm", l_im, y_re, preferred_element_type=jnp.float32
    )
    return jnp.concatenate([s_re, s_im], -1)


def per_device(particles, references, owner_groups, class_order):
    n_cls = lax.axis_size("cls")
    count = particles.shape[0]
    groups = references.shape[0]
    cap = max(2, 2 * count * OWN_TOP // n_cls)
    slots = n_cls * cap
    width = 2 * HARM
    flat_owner = owner_groups.reshape(-1)
    owner_hot = (flat_owner[:, None] == jnp.arange(n_cls, dtype=jnp.int32)[None, :]).astype(
        jnp.int32
    )
    before = jnp.cumsum(owner_hot, axis=0) - owner_hot
    rank = jnp.sum(before * owner_hot, axis=1)
    slot_of = flat_owner * cap + rank
    match = slot_of[None, :] == jnp.arange(slots, dtype=jnp.int32)[:, None]
    member = jnp.any(match.reshape(slots, count, OWN_TOP), axis=2)
    filled = jnp.any(member, axis=1)
    dispatch = member.astype(jnp.bfloat16)
    outgoing = jnp.dot(
        dispatch, particles.reshape(count, CYCLES * width), preferred_element_type=jnp.float32
    )
    outgoing = outgoing.astype(jnp.bfloat16).reshape(n_cls, cap, CYCLES, width)
    match_int = match.astype(jnp.int32)
    picks = class_order[:, :, :CAND_OWN].reshape(count * OWN_TOP, CAND_OWN)
    slot_cand = jnp.where(filled[:, None], jnp.dot(match_int, picks), -1)
    owner_rows = jnp.repeat(jnp.arange(count, dtype=jnp.int32), OWN_TOP)
    slot_pid = jnp.where(filled, jnp.dot(match_int, owner_rows), -1)
    labels_out = jnp.concatenate([slot_cand, slot_pid[:, None]], 1).reshape(
        n_cls, cap, CAND_OWN + 1
    )
    arrived, labels = (
        several_exchanges(outgoing, "cls", 2, 0, 0),
        several_exchanges(labels_out, "cls", 2, 0, 0),
    )
    lanes = arrived.reshape(slots, CYCLES, width)
    labels = labels.reshape(slots, CAND_OWN + 1)
    forward, backward = spectral_tables()
    scale = 2.0 / math.sqrt(CYCLES * width)
    norms = jnp.sum(jnp.square(references.astype(jnp.float32)), axis=(1, 2))
    l_re = lanes[..., :HARM]
    l_im = lanes[..., HARM:]
    r_re = references[..., :HARM]
    r_im = references[..., HARM:]
    x_re = jnp.einsum("lrm,crm->lcm", l_re, r_re, preferred_element_type=jnp.float32) + jnp.einsum(
        "lrm,crm->lcm", l_im, r_im, preferred_element_type=jnp.float32
    )
    x_im = jnp.einsum("lrm,crm->lcm", l_im, r_re, preferred_element_type=jnp.float32) - jnp.einsum(
        "lrm,crm->lcm", l_re, r_im, preferred_element_type=jnp.float32
    )
    cross = jnp.concatenate([x_re, x_im], -1)
    corr = jnp.dot(
        cross.reshape(slots * groups, width), forward, precision=lax.Precision.HIGHEST
    ).reshape(slots, groups, ROTS)
    score = (corr - 0.5 * norms[None, :, None]) * scale
    candidate = jnp.any(
        labels[:, :CAND_OWN, None] == jnp.arange(groups, dtype=jnp.int32)[None, None, :], axis=1
    )
    part_max = jnp.max(jnp.where(candidate[:, :, None], score, lowest), axis=(1, 2))
    part_sum = jnp.sum(
        jnp.where(candidate[:, :, None], jnp.exp(score - part_max[:, None, None]), 0.0), axis=(1, 2)
    )
    sender_ids = labels[:, CAND_OWN].astype(jnp.float32)
    table_max, table_sum, table_ids = side_by_side(
        (
            part_max.reshape(1, n_cls, cap),
            part_sum.reshape(1, n_cls, cap),
            sender_ids.reshape(1, n_cls, cap),
        ),
        "cls",
        0,
        1,
    )
    local_ids = jnp.arange(count, dtype=jnp.float32)
    hit = table_ids[..., None] == local_ids
    top = jnp.max(jnp.where(hit, table_max[..., None], lowest), axis=(0, 2))
    total = jnp.sum(
        jnp.where(
            hit, table_sum[..., None] * jnp.exp(table_max[..., None] - top[None, :, None, :]), 0.0
        ),
        axis=(0, 2),
    )
    table_norm = top + jnp.log(total)
    slot_ids = labels[:, CAND_OWN].reshape(n_cls, cap)
    slot_norm = jnp.sum(
        jnp.where(
            slot_ids[..., None] == jnp.arange(count, dtype=jnp.int32), table_norm[:, None, :], 0.0
        ),
        axis=2,
    ).reshape(slots)
    own_norm = lax.dynamic_index_in_dim(table_norm, lax.axis_index("cls"), 0, keepdims=False)
    weight = jnp.where(candidate[:, :, None], jnp.exp(score - slot_norm[:, None, None]), 0.0)
    mixed = (
        jnp.dot(weight.reshape(slots * groups, ROTS), backward, precision=lax.Precision.HIGHEST)
        .astype(jnp.bfloat16)
        .reshape(slots, groups, width)
    )
    class_weights = taken_together(jnp.sum(weight, axis=(0, 2)), "prt")
    partial_sums = class_accumulate(lanes, mixed)
    class_sums = lax.psum_scatter(partial_sums, "prt", scatter_dimension=1, tiled=True)
    return (class_sums, class_weights, own_norm)


def solution(mesh):
    in_specs = (
        P(("cls", "prt"), None, None),
        P("cls", None, None),
        P(("cls", "prt"), None),
        P(("cls", "prt"), None, None),
    )
    out_specs = (P("cls", "prt", None), P("cls"), P(("cls", "prt")))
    return jax.shard_map(
        per_device, mesh=mesh, in_specs=in_specs, out_specs=out_specs, check_vma=False
    )
```

profile of v0, /device:TPU:1, one launch (start us, length us, event | category | flops | bytes accessed | tf_op | source)
XLA Modules:
  0.0 499.7 jit_solution(66634208029432471)
XLA Ops:
  11.7 8.6 %all-to-all-start = ((s32[32,1,2,5]{3,2,1,0:T(2,128)}), s32[32,1,2,5]{3,2,1,0:T(2,128)S(1)}, u32[]{:S(2)}, u32[]{:S(2)}) async-start(s32[32,1,2,5]{3,2,1,0:T(2,128)} %copy.126), calls=%async_computation | async-start | bytes 65536 | tf_op jit(solution)/shard_map/all_to_all | solution.py:43
  23.1 8.1 %convolution_convert_fusion = bf16[128,65536]{1,0:T(8,128)(2,1)} fusion(pred[128,16]{0,1:T(8,128)(4,1)S(1)} %get-tuple-element.25, bf16[16,65536]{1,0:T(8,128)(2,1)S(1)} %bitcast.66), kind=kOutput, calls=%fused_computation | convolution fusion | flops 276824064 | bytes 18876416 | tf_op jit(solution)/shard_map/dot_general | solution.py:112
  31.2 16.6 %copy.155 = bf16[16,8,128,512]{3,2,1,0:T(8,128)(2,1)} copy(bf16[16,8,128,512]{3,1,2,0:T(8,128)(2,1)} %bitcast.65) | data formatting | bytes 33554432
  48.5 7.4 %all-to-all-start.1 = ((s32[32,1,2,5]{3,2,1,0:T(2,128)}), s32[32,1,2,5]{3,2,1,0:T(2,128)S(1)}, u32[]{:S(2)}, u32[]{:S(2)}) async-start(s32[32,1,2,5]{3,2,1,0:T(2,128)} %copy.127), calls=%async_computation.1 | async-start | bytes 65536 | tf_op jit(solution)/shard_map/all_to_all | solution.py:43
  55.9 11.7 %fusion.38 = (bf16[32,1,4,64,512]{4,3,2,1,0:T(8,128)(2,1)}, bf16[32,1,4,64,512]{4,3,2,1,0:T(8,128)(2,1)}) fusion(bf16[32,1,4,128,512]{4,3,2,1,0:T(8,128)(2,1)} %bitcast.64), kind=kLoop, calls=%fused_computation.70 | loop fusion | bytes 33554432 | tf_op jit(solution)/shard_map/split | solution.py:41
  67.6 103.0 %all_to_all.31 = bf16[32,1,4,64,512]{4,3,2,1,0:T(8,128)(2,1)} all-to-all(bf16[32,1,4,64,512]{4,3,2,1,0:T(8,128)(2,1)} %get-tuple-element.28), channel_id=1, replica_groups=mesh['cls'=32,'prt'=8] {'cls'}, dimensions={0} | all-to-all | bytes 16777216 | tf_op jit(solution)/shard_map/all_to_all | solution.py:43
  170.7 4.9 all-to-all-start.3
  185.9 94.0 %all-to-all-done.3 = bf16[32,1,4,64,512]{4,3,2,1,0:T(8,128)(2,1)} async-done(((bf16[32,1,4,64,512]{4,3,2,1,0:T(8,128)(2,1)}), bf16[32,1,4,64,512]{4,3,2,1,0:T(8,128)(2,1)}, u32[]{:S(2)}, u32[]{:S(2)}) %all-to-all-start.3) | async-done | bytes 8388640 | tf_op jit(solution)/shard_map/all_to_all | solution.py:43
  279.9 13.7 %pad_maximum_fusion = bf16[32,1,4,128,512]{4,3,2,1,0:T(8,128)(2,1)} fusion(bf16[32,1,4,64,512]{4,3,2,1,0:T(8,128)(2,1)} %all-to-all-done.3, bf16[32,1,4,64,512]{4,3,2,1,0:T(8,128)(2,1)} %all_to_all.31), kind=kLoop, calls=%fused_computation.1 | loop fusion | flops 33554432 | bytes 33554432 | tf_op jit(solution)/shard_map/concatenate | solution.py:44
  293.6 28.1 %copy.131 = bf16[32,1,4,128,512]{3,2,0,4,1:T(4,128)(2,1)} copy(bf16[32,1,4,128,512]{4,3,2,1,0:T(8,128)(2,1)} %pad_maximum_fusion) | data formatting | bytes 33554432 | tf_op jit(solution)/shard_map/concatenate | solution.py:44
  321.8 9.1 %fusion.42 = f32[256,128,16]{1,2,0:T(8,128)} fusion(bf16[128,128,512]{1,0,2:T(8,128)(2,1)} %bitcast.56, bf16[16,128,256]{1,0,2:T(8,128)(2,1)S(1)} %copy.148), kind=kOutput, calls=%fused_computation.74 | convolution fusion | flops 134217728 | bytes 19922944 | tf_op jit(solution)/shard_map/lrm,crm->lcm/dot_general | solution.py:137
  330.9 9.3 %fusion.43 = f32[256,128,16]{1,2,0:T(8,128)} fusion(bf16[128,128,512]{1,0,2:T(8,128)(2,1)} %bitcast.57, bf16[16,128,256]{1,0,2:T(8,128)(2,1)S(1)} %copy.148), kind=kOutput, calls=%fused_computation.75 | convolution fusion | flops 134217728 | bytes 19922944 | tf_op jit(solution)/shard_map/lrm,crm->lcm/dot_general | solution.py:140
  340.2 9.3 %add_bitcast_fusion.1 = f32[128,16,256]{0,1,2:T(8,128)} fusion(f32[256,128,16]{1,2,0:T(8,128)S(1)} %copy-done.4, bf16[128,128,512]{1,0,2:T(8,128)(2,1)} %bitcast.58, bf16[16,128,256]{1,0,2:T(8,128)(2,1)S(1)} %copy-done), kind=kOutput, calls=%fused_computation.19 | convolution fusion | flops 134742016 | bytes 22020096 | tf_op jit(solution)/shard_map/lrm,crm->lcm/dot_general | solution.py:137
  349.5 8.0 %subtract_bitcast_fusion.1 = f32[128,16,256]{0,1,2:T(8,128)S(1)} fusion(f32[256,128,16]{1,2,0:T(8,128)S(1)} %copy-done.3, bf16[128,128,512]{1,0,2:T(8,128)(2,1)} %bitcast.59, bf16[16,128,256]{1,0,2:T(8,128)(2,1)S(1)} %copy-done), kind=kOutput, calls=%fused_computation.18 | convolution fusion | flops 134742016 | bytes 22020096 | tf_op jit(solution)/shard_map/lrm,crm->lcm/dot_general | solution.py:140
  363.6 27.5 %all-to-all-start.4 = ((f32[32,1,96,4]{2,3,1,0:T(4,128)}), f32[32,1,96,4]{2,3,1,0:T(4,128)S(1)}, u32[]{:S(2)}, u32[]{:S(2)}) async-start(f32[32,1,96,4]{2,3,1,0:T(4,128)} %broadcast_in_dim.113), calls=%async_computation.4 | async-start | bytes 131072 | tf_op jit(solution)/shard_map/all_to_all | solution.py:49
  391.3 7.1 %all-to-all-done.4 = f32[32,1,96,4]{2,3,1,0:T(4,128)S(1)} async-done(((f32[32,1,96,4]{2,3,1,0:T(4,128)}), f32[32,1,96,4]{2,3,1,0:T(4,128)S(1)}, u32[]{:S(2)}, u32[]{:S(2)}) %all-to-all-start.4) | async-done | bytes 49184 | tf_op jit(solution)/shard_map/all_to_all | solution.py:49
  405.5 7.0 %fusion = f32[256,16,128]{2,1,0:T(8,128)} fusion(bf16[128,16,256]{0,1,2:T(8,128)(2,1)S(1)} %copy.152, bf16[128,128,512]{1,0,2:T(8,128)(2,1)} %bitcast.60), kind=kOutput, calls=%fused_computation.2 | convolution fusion | flops 134217728 | bytes 11534336 | tf_op jit(solution)/shard_map/lrm,lcm->crm/dot_general | solution.py:85
  414.2 4.8 fusion.2
  419.0 4.7 subtract_bitcast_fusion
  423.7 4.7 add_bitcast_fusion
  430.7 5.6 %copy.143 = f32[16,128,512]{2,0,1:T(8,128)} copy(f32[16,128,512]{1,0,2:T(8,128)} %pad_maximum_fusion.2) | data formatting | bytes 8388608 | tf_op jit(solution)/shard_map/concatenate | solution.py:91
  436.9 8.2 %all-to-all-start.5 = ((f32[8,1,16]{2,1,0:T(1,128)}), f32[8,1,16]{2,1,0:T(1,128)S(1)}, u32[]{:S(2)}, u32[]{:S(2)}) async-start(f32[8,1,16]{2,1,0:T(1,128)} %broadcast_in_dim.119), calls=%async_computation.6 | async-start | bytes 8192 | tf_op jit(solution)/shard_map/all_to_all | solution.py:49
  445.8 5.8 %all-to-all-done.5 = f32[8,1,16]{2,1,0:T(1,128)S(1)} async-done(((f32[8,1,16]{2,1,0:T(1,128)}), f32[8,1,16]{2,1,0:T(1,128)S(1)}, u32[]{:S(2)}, u32[]{:S(2)}) %all-to-all-start.5) | async-done | bytes 544 | tf_op jit(solution)/shard_map/all_to_all | solution.py:49
  452.1 38.6 %reduce-scatter.2.cloned.1.call-done = f32[16,16,512]{2,0,1:T(8,128)} async-done(((f32[16,128,512]{2,0,1:T(8,128)}), f32[16,16,512]{2,0,1:T(8,128)}) %reduce-scatter.2.cloned.1.call-update) | async-done | bytes 524304 | tf_op jit(solution)/shard_map/reduce_scatter | solution.py:192
  (96 shorter events, 39.4 us)
Async XLA Ops:
  11.7 36.8 %all-to-all-start = ((s32[32,1,2,5]{3,2,1,0:T(2,128)}), s32[32,1,2,5]{3,2,1,0:T(2,128)S(1)}, u32[]{:S(2)}, u32[]{:S(2)}) async-start(s32[32,1,2,5]{3,2,1,0:T(2,128)} %copy.126), calls=%async_computation | async-start | bytes 65536 | tf_op jit(solution)/shard_map/all_to_all | solution.py:43
  48.5 19.1 %all-to-all-start.1 = ((s32[32,1,2,5]{3,2,1,0:T(2,128)}), s32[32,1,2,5]{3,2,1,0:T(2,128)S(1)}, u32[]{:S(2)}, u32[]{:S(2)}) async-start(s32[32,1,2,5]{3,2,1,0:T(2,128)} %copy.127), calls=%async_computation.1 | async-start | bytes 65536 | tf_op jit(solution)/shard_map/all_to_all | solution.py:43
  170.7 4.9 copy-start.1
  170.7 109.2 %all-to-all-start.3 = ((bf16[32,1,4,64,512]{4,3,2,1,0:T(8,128)(2,1)}), bf16[32,1,4,64,512]{4,3,2,1,0:T(8,128)(2,1)}, u32[]{:S(2)}, u32[]{:S(2)}) async-start(bf16[32,1,4,64,512]{4,3,2,1,0:T(8,128)(2,1)} %get-tuple-element.29), calls=%async_computation.3 | async-start | bytes 16777216 | tf_op jit(solution)/shard_map/all_to_all | solution.py:43
  330.9 9.3 %copy-start = (bf16[16,128,256]{1,0,2:T(8,128)(2,1)S(1)}, bf16[16,128,256]{1,0,2:T(8,128)(2,1)}, u32[]{:S(2)}) copy-start(bf16[16,128,256]{1,0,2:T(8,128)(2,1)} %copy.149) | copy-start | bytes 3145732
  330.9 9.3 %copy-start.4 = (f32[256,128,16]{1,2,0:T(8,128)S(1)}, f32[256,128,16]{1,2,0:T(8,128)}, u32[]{:S(2)}) copy-start(f32[256,128,16]{1,2,0:T(8,128)} %fusion.42) | copy-start | bytes 6291460
  340.2 9.3 %copy-start.3 = (f32[256,128,16]{1,2,0:T(8,128)S(1)}, f32[256,128,16]{1,2,0:T(8,128)}, u32[]{:S(2)}) copy-start(f32[256,128,16]{1,2,0:T(8,128)} %fusion.43) | copy-start | bytes 6291460
  349.5 8.0 %copy-start.5 = (f32[128,16,256]{0,1,2:T(8,128)S(1)}, f32[128,16,256]{0,1,2:T(8,128)}, u32[]{:S(2)}) copy-start(f32[128,16,256]{0,1,2:T(8,128)} %add_bitcast_fusion.1) | copy-start | bytes 6291460
  357.6 0.8 copy-start.6
  357.6 0.8 copy-start.7
  357.6 0.8 copy-start.9
  357.6 0.8 copy-start.12
  357.9 5.0 %copy-start.10 = (f32[1,32,4]{1,2,0:T(4,128)S(1)}, f32[1,32,4]{1,2,0:T(4,128)}, u32[]{:S(2)}) copy-start(f32[1,32,4]{1,2,0:T(4,128)} %copy.138) | copy-start | bytes 1540
  357.9 33.3 %copy-start.11 = (s32[128]{0:T(128)S(1)}, s32[128]{0:T(128)}, u32[]{:S(2)}) copy-start(s32[128]{0:T(128)} %get-tuple-element.34) | copy-start | bytes 1540
  357.9 42.2 %copy-start.8 = (f32[256,36]{0,1:T(8,128)S(1)}, f32[256,36]{0,1:T(8,128)}, u32[]{:S(2)}) copy-start(f32[256,36]{0,1:T(8,128)} %get-tuple-element.41) | copy-start | bytes 110596
  363.6 34.8 %all-to-all-start.4 = ((f32[32,1,96,4]{2,3,1,0:T(4,128)}), f32[32,1,96,4]{2,3,1,0:T(4,128)S(1)}, u32[]{:S(2)}, u32[]{:S(2)}) async-start(f32[32,1,96,4]{2,3,1,0:T(4,128)} %broadcast_in_dim.113), calls=%async_computation.4 | async-start | bytes 131072 | tf_op jit(solution)/shard_map/all_to_all | solution.py:49
  391.1 99.6 %reduce-scatter.2.cloned.1.call-start = ((), (), s32[]{:S(2)}) async-start(), calls=%async_computation.7 | async-start | bytes 4718592 | tf_op jit(solution)/shard_map/reduce_scatter | solution.py:192
  414.2 4.8 copy-start.2
  436.9 14.7 %all-to-all-start.5 = ((f32[8,1,16]{2,1,0:T(1,128)}), f32[8,1,16]{2,1,0:T(1,128)S(1)}, u32[]{:S(2)}, u32[]{:S(2)}) async-start(f32[8,1,16]{2,1,0:T(1,128)} %broadcast_in_dim.119), calls=%async_computation.6 | async-start | bytes 8192 | tf_op jit(solution)/shard_map/all_to_all | solution.py:49
Sparse Core Ops, SparseCore 0:
  436.4 54.2 reduce-scatter.1
where the time goes:
time: 501 us; the launch traced here: 500 us
  waiting for transfers between devices  145 us (29%)
  blocking collectives  103 us (21%)
  local copies, waits for them, and re-layouts  85 us (17%)
  matrix products  73.8 us (15%)
  starting transfers between devices  56.5 us (11%)
  other arithmetic  21.5 us (4%)
  between operations  14.3 us (3%)
    all_to_all x1, blocking collectives, several_exchanges(): lax.all_to_all(slab, axis, split_axis=0, concat_axis=0, tiled=True)  103 us
    all_to_all x3, waiting for transfers between devices, several_exchanges(): lax.all_to_all(slab, axis, split_axis=0, concat_axis=0, tiled=True)  94 us
    reduce_scatter x1, waiting for transfers between devices, per_device(): lax.psum_scatter(partial_sums, 'prt', scatter_dimension=1, tiled=True)  38.6 us
    all_to_all x2, starting transfers between devices, sent_to_all(): lax.all_to_all(jnp.broadcast_to(x[None], (devices, *x.shape)), axis, 0, 0...  35.6 us
    unnamed x37, local copies, waits for them, and re-layouts  31.5 us
    concatenate x1, local copies, waits for them, and re-layouts, several_exchanges(): return joined_along(jnp.concatenate(outs, axis=widest), concat_dim)  28.1 us
    all_to_all x3, starting transfers between devices, several_exchanges(): lax.all_to_all(slab, axis, split_axis=0, concat_axis=0, tiled=True)  20.8 us
    concatenate x2, other arithmetic, several_exchanges(): return joined_along(jnp.concatenate(outs, axis=widest), concat_dim)  13.8 us
  transfers between devices with their start and end apart: 6, of which 4 were waited for; matrix products, arithmetic and copies ran while one was open for 10% of the time, Pallas kernels for 0%

commit v1 on v0

v1 whole, which is shorter than its diff:
```python
import functools
import math

import jax
import jax.numpy as jnp
from jax import lax
from jax.experimental import pallas as pl
from jax.experimental.pallas import tpu as pltpu
from jax.sharding import PartitionSpec as P

CYCLES = 128
HARM = 256
ROTS = 36
OWN_TOP = 4
CAND_OWN = 4
VMEM = pltpu.VMEM


def spectral_tables():
    harmonic = jnp.arange(HARM, dtype=jnp.float32)
    angles = 2.0 * math.pi * jnp.arange(ROTS, dtype=jnp.float32) / ROTS
    phase = harmonic[:, None] * angles[None, :]
    forward = jnp.concatenate([jnp.cos(phase), jnp.sin(phase)], 0)
    backward = jnp.concatenate([jnp.cos(phase), -jnp.sin(phase)], 0).T
    return (forward, backward)


def cross_kernel(cands, cand_ref, p_ref, r_ref, fwd_ref, corr_ref, cross, normrow, norms):
    n_part = p_ref.shape[0]

    @pl.loop(0, r_ref.shape[0] // 8)
    def _(b):
        rows = []
        for i in range(8):
            r = r_ref[b * 8 + i].astype(jnp.float32)
            s = jnp.sum(r * r, axis=0, keepdims=True)
            s = s[:, :HARM] + s[:, HARM:]
            rows.append(s[:, :128] + s[:, 128:])
        norms[pl.ds(b * 8, 8), :] = jnp.broadcast_to(
            0.5 * jnp.sum(jnp.concatenate(rows, 0), axis=1, keepdims=True), (8, 128)
        )

    @pl.loop(0, n_part)
    def _(n):
        p = p_ref[n].astype(jnp.float32)
        p_re, p_im = p[:, :HARM], p[:, HARM:]
        for j in range(cands):
            c = cand_ref[n * cands + j]
            r = r_ref[c].astype(jnp.float32)
            r_re, r_im = r[:, :HARM], r[:, HARM:]
            a = p_re * r_re + p_im * r_im
            b = p_im * r_re - p_re * r_im
            cross[pl.ds(n * cands + j, 1), :HARM] = jnp.sum(a, axis=0, keepdims=True)
            cross[pl.ds(n * cands + j, 1), HARM:] = jnp.sum(b, axis=0, keepdims=True)
            normrow[pl.ds(n * cands + j, 1), :] = norms[pl.ds(c, 1), :]

    @pl.loop(0, cross.shape[0] // 256)
    def _(b):
        rows = pl.ds(pl.multiple_of(b * 256, 256), 256)
        corr_ref[rows, :] = (
            jnp.dot(cross[rows, :], fwd_ref[...], precision=lax.Precision.HIGHEST)
            - normrow[rows, :]
        )


def sums_kernel(cands, cand_ref, p_ref, w_ref, bwd_ref, acc_ref, accw_ref, mixed):
    n_part = p_ref.shape[0]

    @pl.loop(0, mixed.shape[0] // 256)
    def _(b):
        rows = pl.ds(pl.multiple_of(b * 256, 256), 256)
        mixed[rows, :] = (
            jnp.dot(w_ref[rows, :], bwd_ref[...], precision=lax.Precision.HIGHEST)
            .astype(jnp.bfloat16)
            .astype(jnp.float32)
        )

    @pl.loop(0, acc_ref.shape[0])
    def _(c):
        acc_ref[c] = jnp.zeros(acc_ref.shape[1:], jnp.float32)

    accw_ref[...] = jnp.zeros_like(accw_ref)

    @pl.loop(0, n_part)
    def _(n):
        p = p_ref[n].astype(jnp.float32)
        p_re, p_im = p[:, :HARM], p[:, HARM:]
        for j in range(cands):
            c = cand_ref[n * cands + j]
            y = mixed[pl.ds(n * cands + j, 1), :]
            y_re, y_im = y[:, :HARM], y[:, HARM:]
            acc_ref[c, :, :HARM] += p_re * y_re - p_im * y_im
            acc_ref[c, :, HARM:] += p_re * y_im + p_im * y_re
            accw_ref[pl.ds(c, 1), :] += w_ref[pl.ds(n * cands + j, 1), :]


def per_device(particles, references, owner_groups, class_order):
    n_prt = lax.axis_size("prt")
    z = lax.axis_index("prt")
    count = particles.shape[0]
    groups = references.shape[0]
    width = 2 * HARM
    depth = CYCLES // n_prt
    cands = OWN_TOP * CAND_OWN
    total = count * n_prt
    classes = groups * lax.axis_size("cls")
    scale = 2.0 / math.sqrt(CYCLES * width)
    forward, backward = spectral_tables()
    fwd = jnp.pad(forward, ((0, 0), (0, 128 - ROTS)))
    bwd = jnp.pad(backward, ((0, 128 - ROTS), (0, 0)))

    own_cand = (owner_groups[:, :, None] * groups + class_order[:, :, :CAND_OWN]).reshape(-1)
    cand = lax.all_gather(own_cand, "prt", axis=0, tiled=True)
    column = lax.all_to_all(
        particles.reshape(count, n_prt, depth, width), "prt", split_axis=1, concat_axis=0, tiled=True
    ).reshape(total, depth, width)
    slab = lax.dynamic_slice_in_dim(references, z * depth, depth, axis=1)
    refs = lax.all_gather(slab, "cls", axis=0, tiled=True)

    corr = pl.pallas_call(
        functools.partial(cross_kernel, cands),
        out_shape=jax.ShapeDtypeStruct((total * cands, 128), jnp.float32),
        in_specs=[pl.BlockSpec(memory_space=pltpu.SMEM)] + [pl.BlockSpec(memory_space=VMEM)] * 3,
        out_specs=pl.BlockSpec(memory_space=VMEM),
        scratch_shapes=[
            VMEM((total * cands, width), jnp.float32),
            VMEM((total * cands, 128), jnp.float32),
            VMEM((classes, 128), jnp.float32),
        ],
        compiler_params=pltpu.CompilerParams(vmem_limit_bytes=60 * 2**20),
    )(cand, column, refs, fwd)
    mine = lax.psum_scatter(corr[:, :ROTS], "prt", scatter_dimension=0, tiled=True)
    score = mine.reshape(count, cands * ROTS) * scale
    top = jnp.max(score, axis=1, keepdims=True)
    log_norm = top + jnp.log(jnp.sum(jnp.exp(score - top), axis=1, keepdims=True))
    weight = jnp.exp(score - log_norm).reshape(count * cands, ROTS)
    weights = lax.all_gather(weight, "prt", axis=0, tiled=True)
    sums, sums_w = pl.pallas_call(
        functools.partial(sums_kernel, cands),
        out_shape=(
            jax.ShapeDtypeStruct((classes, depth, width), jnp.float32),
            jax.ShapeDtypeStruct((classes, 128), jnp.float32),
        ),
        in_specs=[pl.BlockSpec(memory_space=pltpu.SMEM)] + [pl.BlockSpec(memory_space=VMEM)] * 3,
        out_specs=[pl.BlockSpec(memory_space=VMEM)] * 2,
        scratch_shapes=[VMEM((total * cands, width), jnp.float32)],
        compiler_params=pltpu.CompilerParams(vmem_limit_bytes=60 * 2**20),
    )(cand, column, jnp.pad(weights, ((0, 0), (0, 128 - ROTS))), bwd)
    class_sums = lax.psum_scatter(sums, "cls", scatter_dimension=0, tiled=True)
    class_weights = lax.psum_scatter(
        jnp.sum(sums_w, axis=1), "cls", scatter_dimension=0, tiled=True
    )
    return (class_sums, class_weights, log_norm.reshape(count))


def solution(mesh):
    in_specs = (
        P(("cls", "prt"), None, None),
        P("cls", None, None),
        P(("cls", "prt"), None),
        P(("cls", "prt"), None, None),
    )
    out_specs = (P("cls", "prt", None), P("cls"), P(("cls", "prt")))
    return jax.shard_map(
        per_device, mesh=mesh, in_specs=in_specs, out_specs=out_specs, check_vma=False
    )
```

time: 501 us -> 346 us (0.69)
  local copies, waits for them, and re-layouts: 85 us -> 10.6 us
  matrix products: 73.8 us -> 0 us
  Pallas kernels: 0 us -> 66.2 us
  waiting for transfers between devices: 145 us -> 91 us
  starting transfers between devices: 56.5 us -> 9.25 us
  blocking collectives: 103 us -> 150 us
  other arithmetic: 21.5 us -> 3.85 us
    all_to_all x5 -> x1, waiting for transfers between devices: 107 us -> 0.01 us  [per_device(): lax.all_to_all(particles.reshape(count, n_prt, depth, width), 'prt', spli...]
    all_to_all x1 -> x0, blocking collectives: 103 us -> none  [several_exchanges(): lax.all_to_all(slab, axis, split_axis=0, concat_axis=0, tiled=True)]
    all_gather x0 -> x2, blocking collectives: none -> 76.1 us  [the longest x1 55 us: per_device(): cand = lax.all_gather(own_cand, 'prt', axis=0, tiled=True)]
    dot_general x13 -> x0, matrix products: 73.8 us -> none  [the longest x1 9.32 us: per_device(): jnp.einsum('lrm,crm->lcm', l_im, r_im, preferred_element_type=jnp.float32)]
    unnamed x0 -> x1, blocking collectives: none -> 73.4 us
    pallas_call x0 -> x2, Pallas kernels: none -> 66.2 us  [the longest x1 37.6 us: per_device(): pl.pallas_call(functools.partial(cross_kernel, cands), out_shape=jax.Shap...]
    reduce_scatter x1 -> x2, waiting for transfers between devices: 38.6 us -> 90.9 us  [the longest x1 54.8 us: per_device(): class_sums = lax.psum_scatter(sums, 'cls', scatter_dimension=0, tiled=True)]
    all_to_all x5 -> x1, starting transfers between devices: 56.5 us -> 9.13 us  [per_device(): lax.all_to_all(particles.reshape(count, n_prt, depth, width), 'prt', spli...]
  transfers between devices with their start and end apart: 6 -> 4, of which waited for: 4 -> 2; matrix products, arithmetic and copies ran while one was open for 10% -> 2% of each run, Pallas kernels for 0% -> 0%
where the time goes in v1:
time: 346 us; the launch traced here: 345 us
  blocking collectives  150 us (43%)
  waiting for transfers between devices  91 us (26%)
  Pallas kernels  66.2 us (19%)
  between operations  14.5 us (4%)
  local copies, waits for them, and re-layouts  10.6 us (3%)
  starting transfers between devices  9.25 us (3%)
  other arithmetic  3.85 us (1%)
    unnamed x1, blocking collectives  73.4 us
    all_gather x1, blocking collectives, per_device(): cand = lax.all_gather(own_cand, 'prt', axis=0, tiled=True)  55 us
    reduce_scatter x1, waiting for transfers between devices, per_device(): class_sums = lax.psum_scatter(sums, 'cls', scatter_dimension=0, tiled=True)  54.8 us
    pallas_call x1, Pallas kernels, per_device(): pl.pallas_call(functools.partial(cross_kernel, cands), out_shape=jax.Shap...  37.6 us
    reduce_scatter x1, waiting for transfers between devices, per_device(): lax.psum_scatter(corr[:, :ROTS], 'prt', scatter_dimension=0, tiled=True)  36.1 us
    pallas_call x1, Pallas kernels, per_device(): pl.pallas_call(functools.partial(sums_kernel, cands), out_shape=(jax.Shap...  28.6 us
    all_gather x1, blocking collectives, per_device(): weights = lax.all_gather(weight, 'prt', axis=0, tiled=True)  21.2 us
    all_to_all x1, starting transfers between devices, per_device(): lax.all_to_all(particles.reshape(count, n_prt, depth, width), 'prt', spli...  9.13 us
  transfers between devices with their start and end apart: 4, of which 2 were waited for; matrix products, arithmetic and copies ran while one was open for 2% of the time, Pallas kernels for 0%

profile of v1, /device:TPU:1, one launch (start us, length us, event | category | flops | bytes accessed | tf_op | source)
XLA Modules:
  0.0 344.9 jit_solution(8879067002183473713)
XLA Ops:
  7.2 1.5 copy-done
  8.8 0.7 constant_dynamic-slice_fusion
  9.5 3.2 copy.17
  12.7 9.1 %all-to-all-start = ((bf16[16,8,16,512]{3,2,0,1:T(8,128)(2,1)}), bf16[16,8,16,512]{3,2,0,1:T(8,128)(2,1)}, u32[]{:S(2)}, u32[]{:S(2)}) async-start(bf16[16,8,16,512]{3,2,0,1:T(8,128)(2,1)} %copy.17), calls=%async_computation | async-start | bytes 4194304 | tf_op jit(solution)/shard_map/all_to_all | solution.py:114
  21.9 0.2 fusion.3
  22.2 0.1 copy.19
  22.6 0.7 pad.12.clone.fwd_ref
  23.4 55.0 %all-gather = s32[8,1,256]{2,1,0:T(1,128)} all-gather(s32[1,1,256]{2,1,0:T(1,128)S(1)} %reshape.41), channel_id=1, replica_groups=mesh['cls'=32,'prt'=8] {'prt'}, dimensions={0}, use_global_device_ids=true | all-gather | bytes 9216 | tf_op jit(solution)/shard_map/all_gather | solution.py:113
  78.3 37.6 %shard_map.67 = f32[2048,128]{1,0:T(8,128)} custom-call(s32[2048]{0:T(1024)} %bitcast.13, bf16[128,16,512]{2,1,0:T(8,128)(2,1)} %bitcast.4.p_ref, bf16[512,16,512]{2,1,0:T(8,128)(2,1)} %all-gather.3.cloned.1.call-done.r_ref, f32[512,128]{1,0:T(8,128)} %pad.12.clone.fwd_ref), custom_call_target="tpu_custom_call" | custom-call | tf_op jit(solution)/shard_map/pallas_call | solution.py:120
  116.0 0.7 pad.14.bwd_ref
  116.7 36.1 %reduce-scatter.3.cloned.1.call-done = f32[256,36]{1,0:T(8,128)} async-done(((f32[2048,36]{1,0:T(8,128)}), f32[256,36]{1,0:T(8,128)}) %reduce-scatter.3.cloned.1.call-update) | async-done | bytes 36880 | tf_op jit(solution)/shard_map/reduce_scatter | solution.py:132
  152.8 1.0 multiply_reduce_fusion
  153.9 0.1 reduce_max.18
  154.2 1.1 exponential_reduce_fusion
  155.7 1.0 subtract_exponential_fusion
  156.7 21.2 %all_gather.11 = f32[2048,36]{1,0:T(8,128)S(1)} all-gather(f32[256,36]{1,0:T(8,128)S(1)} %subtract_exponential_fusion), channel_id=1, replica_groups=mesh['cls'=32,'prt'=8] {'prt'}, dimensions={0}, use_global_device_ids=true | all-gather | bytes 331776 | tf_op jit(solution)/shard_map/all_gather | solution.py:137
  177.9 1.1 pad.13.w_ref
  178.9 28.6 %shard_map.68 = (f32[512,16,512]{2,1,0:T(8,128)}, f32[512,128]{1,0:T(8,128)}) custom-call(s32[2048]{0:T(1024)} %bitcast.14, bf16[128,16,512]{2,1,0:T(8,128)(2,1)} %bitcast.4.p_ref, f32[2048,128]{1,0:T(8,128)} %pad.13.w_ref, f32[128,512]{1,0:T(8,128)} %pad.14.bwd_ref), custom_call_target="tpu_custom_call" | custom-call | tf_op jit(solution)/shard_map/pallas_call | solution.py:138
  207.6 0.6 copy-done.5
  208.2 0.6 dynamic-slice
  209.5 0.1 reduce_sum.28
  209.6 73.4 %all-reduce.3 = f32[512]{0:T(512)S(1)} all-reduce(f32[512]{0:T(512)S(1)} %reduce_sum.28), channel_id=4, replica_groups=mesh['cls'=32,'prt'=8] {'cls'}, use_global_device_ids=true, to_apply=%region_7.8.clone | all-reduce | flops 512 | bytes 4096
  283.0 0.6 dynamic-slice.1
  283.6 54.8 %reduce-scatter.5.cloned.1.call-done = f32[16,16,512]{2,1,0:T(8,128)} async-done(((f32[512,16,512]{2,1,0:T(8,128)}), f32[16,16,512]{2,1,0:T(8,128)}) %reduce-scatter.5.cloned.1.call-update) | async-done | bytes 524304 | tf_op jit(solution)/shard_map/reduce_scatter | solution.py:149
  (32 shorter events, 1.1 us)
Async XLA Ops:
  7.2 1.6 copy-start
  7.2 71.2 %all-gather.3.cloned.1.call-start = ((), (), s32[]{:S(2)}) async-start(), calls=%async_computation.3 | async-start | bytes 8650752 | tf_op jit(solution)/shard_map/all_gather | solution.py:118
  12.7 9.6 %copy-start.3 = (s32[16,4]{0,1:T(4,128)S(1)}, s32[16,4]{0,1:T(4,128)}, u32[]{:S(2)}) copy-start(s32[16,4]{0,1:T(4,128)} %param.6) | copy-start | bytes 772
  12.7 9.7 %copy-start.2 = (s32[16,4,16]{2,1,0:T(4,128)S(1)}, s32[16,4,16]{2,1,0:T(4,128)}, u32[]{:S(2)}) copy-start(s32[16,4,16]{2,1,0:T(4,128)} %param.7) | copy-start | bytes 12292
  12.7 65.6 %all-to-all-start = ((bf16[16,8,16,512]{3,2,0,1:T(8,128)(2,1)}), bf16[16,8,16,512]{3,2,0,1:T(8,128)(2,1)}, u32[]{:S(2)}, u32[]{:S(2)}) async-start(bf16[16,8,16,512]{3,2,0,1:T(8,128)(2,1)} %copy.17), calls=%async_computation | async-start | bytes 4194304 | tf_op jit(solution)/shard_map/all_to_all | solution.py:114
  21.9 131.0 %reduce-scatter.3.cloned.1.call-start = ((), (), s32[]{:S(2)}) async-start(), calls=%async_computation.4 | async-start | bytes 1179648 | tf_op jit(solution)/shard_map/reduce_scatter | solution.py:132
  115.9 222.5 %reduce-scatter.5.cloned.1.call-start = ((), (), s32[]{:S(2)}) async-start(), calls=%async_computation.5 | async-start | bytes 17301504 | tf_op jit(solution)/shard_map/reduce_scatter | solution.py:149
  155.5 52.0 %copy-start.4 = (f32[16]{0:T(128)}, f32[16]{0:T(128)S(1)}, u32[]{:S(2)}) copy-start(f32[16]{0:T(128)S(1)} %log_add_fusion) | copy-start | bytes 196
  207.5 0.7 copy-start.5
  207.5 1.9 copy-start.1
Sparse Core Ops, SparseCore 0:
  11.1 61.8 all-gather.2
  116.1 36.7 reduce-scatter.2
  207.7 130.6 reduce-scatter.4

commit v2 on v1

v2 whole, which is shorter than its diff:
```python
import functools
import math

import jax
import jax.numpy as jnp
import numpy as np
from jax import lax
from jax.experimental import pallas as pl
from jax.experimental.pallas import tpu as pltpu
from jax.sharding import PartitionSpec as P

CYCLES = 128
HARM = 256
WIDTH = 2 * HARM
ROTS = 36
OWN_TOP = 4
CAND_OWN = 4
CANDS = OWN_TOP * CAND_OWN
ANG = 40
EXT = WIDTH + 128
VMEM, SMEM, ANY = pltpu.VMEM, pltpu.SMEM, pl.ANY
F32, BF16 = jnp.float32, jnp.bfloat16
DMA = pltpu.SemaphoreType.DMA
SCALE = 2.0 / math.sqrt(CYCLES * WIDTH)


def split3(x):
    high = x.astype(jnp.bfloat16).astype(np.float32)
    mid = (x - high).astype(jnp.bfloat16).astype(np.float32)
    low = (x - high - mid).astype(jnp.bfloat16).astype(np.float32)
    return high, mid, low


def spectral_tables():
    harmonic = np.arange(HARM, dtype=np.float32)
    angles = np.float32(2.0 * math.pi) * np.arange(ROTS, dtype=np.float32) / np.float32(ROTS)
    phase = (harmonic[:, None] * angles[None, :]).astype(np.float64)
    cos, sin = np.cos(phase).astype(np.float32).T, np.sin(phase).astype(np.float32).T
    forward = np.zeros((ANG, EXT), np.float32)
    forward[:ROTS, :HARM], forward[:ROTS, HARM:WIDTH] = cos, sin
    forward[:ROTS, WIDTH:] = -0.5
    backward = np.zeros((ANG, EXT), np.float32)
    backward[:ROTS, :HARM], backward[:ROTS, HARM:WIDTH] = cos, -sin
    backward[:ROTS, WIDTH:] = 1.0
    f_high, f_mid, f_low = split3(forward)
    b_high, b_mid, b_low = split3(backward)
    fwd = np.concatenate([f_high, f_mid, f_low, np.zeros((8, EXT), np.float32)], 0)
    bwd = np.concatenate([b_high, b_high, b_high, b_mid, b_mid, b_low], 0)
    return jnp.asarray(fwd, BF16), jnp.asarray(bwd, BF16)


def parts3(x):
    high = x.astype(BF16)
    rest = x - high.astype(F32)
    mid = rest.astype(BF16)
    low = (rest - mid.astype(F32)).astype(BF16)
    return high, mid, low


def row_sums(vs):
    row = lax.broadcasted_iota(jnp.int32, vs[0].shape, 0)
    for step in (1, 2, 4):
        keep = (row % (2 * step)) < step
        vs = [
            jnp.where(keep, a, b) + pltpu.roll(jnp.where(keep, b, a), 8 - step, 0)
            for a, b in zip(vs[0::2], vs[1::2])
        ]
    return vs[0]


def group_all(x, op):
    lane = lax.broadcasted_iota(jnp.int32, x.shape, 1)
    n = x.shape[1]
    for step in (1, 2, 4, 8):
        other = jnp.where(
            (lane // step) % 2 == 0, pltpu.roll(x, n - step, 1), pltpu.roll(x, step, 1)
        )
        x = op(x, other)
    return x


def where_am_i():
    cls = lax.axis_index("cls")
    return cls // 8, (cls // 2) % 4, cls % 2, lax.axis_index("prt")


def cls_of(x, y, core):
    return (x % 4) * 8 + (y % 4) * 2 + core


def remote(src, dst, send, recv, cls, prt):
    return pltpu.make_async_remote_copy(
        src, dst, send, recv, device_id=(cls, prt), device_id_type=pl.DeviceIdType.MESH
    )


def greet(peers):
    barrier = pltpu.get_barrier_semaphore()
    for cls, prt in peers:
        pl.semaphore_signal(
            barrier, inc=1, device_id=(cls, prt), device_id_type=pl.DeviceIdType.MESH
        )
    pl.semaphore_wait(barrier, len(peers))


def assign_kernel(
    part, refs, cand, fwd,
    halves, weights, cand_out, lse_out,
    pbuf, rbuf, cbuf, csm, cross, normrow, norms, cout, cin, wown,
    lsem, psend, precv, csend, crecv, r1send, r1recv, r2send, r2recv, rsend, rrecv,
    csem_s, csem_r, wsend, wrecv, xsend, xrecv,
):
    x, y, core, z = where_am_i()
    me = cls_of(x, y, core)
    mate = cls_of(x, y, 1 - core)
    greet(
        [(me, (z + d) % 8) for d in range(1, 8)]
        + [(cls_of(x + d, y, core), z) for d in range(1, 4)]
        + [(cls_of(x, y + d, core), z) for d in range(1, 4)]
        + [(mate, z)]
    )
    order = (1, 7, 2, 6, 3, 5, 4)

    c_cp = [remote(cand, cbuf.at[z], csend.at[d], crecv.at[d], me, (z + d) % 8) for d in order]
    for cp in c_cp:
        cp.start()

    def slab(g):
        return rbuf.at[pl.ds(g * 16, 16)]

    def half(g, k):
        return rbuf.at[pl.ds(g * 16 + 8 * k, 8)]

    r_cp = []
    for d in (1, 3, 2):
        r_cp.append(remote(refs.at[:, z], slab(me), r1send.at[d - 1], r1recv.at[d - 1], cls_of(x + d, y, core), z))
        r_cp.append(remote(refs.at[:, z], slab(me), r1send.at[d + 2], r1recv.at[d + 2], cls_of(x, y + d, core), z))
    r_cp.append(remote(refs.at[:, z], slab(me), rsend.at[0], rrecv.at[0], mate, z))
    p_cp = [remote(part.at[:, (z + d) % 8], pbuf.at[z], psend.at[d], precv.at[d], me, (z + d) % 8) for d in order]
    for cp in r_cp + p_cp:
        cp.start()
    own = [
        pltpu.make_async_copy(cand, cbuf.at[z], lsem.at[0]),
        pltpu.make_async_copy(refs.at[:, z], slab(me), lsem.at[1]),
        pltpu.make_async_copy(part.at[:, z], pbuf.at[z], lsem.at[2]),
    ]
    for cp in own:
        cp.start()

    sent = []

    def pass_on(ref, send, recv, cls):
        cp = remote(ref, ref, send, recv, cls, z)
        cp.start()
        sent.append(cp)

    for d in (1, 3, 2):
        g = cls_of(x - d + 4, y, core)
        remote(slab(g), slab(g), r1send.at[d - 1], r1recv.at[d - 1], me, z).wait_recv()
        for e in (1, 3, 2):
            k = (d - 1) * 3 + e - 1
            pass_on(half(g, 0), r2send.at[0, k], r2recv.at[0, k], cls_of(x, y + e, core))
        pass_on(slab(g), rsend.at[4 * d], rrecv.at[4 * d], mate)
        g = cls_of(x, y - d + 4, core)
        remote(slab(g), slab(g), r1send.at[d + 2], r1recv.at[d + 2], me, z).wait_recv()
        for e in (1, 3, 2):
            k = (e - 1) * 3 + d - 1
            pass_on(half(g, 1), r2send.at[1, k], r2recv.at[1, k], cls_of(x + e, y, core))
        pass_on(slab(g), rsend.at[d], rrecv.at[d], mate)
    for dx in (1, 3, 2):
        for dy in (1, 3, 2):
            k = (dx - 1) * 3 + dy - 1
            g = cls_of(x - dx + 4, y - dy + 4, core)
            for h in range(2):
                remote(half(g, h), half(g, h), r2send.at[h, k], r2recv.at[h, k], me, z).wait_recv()
            pass_on(slab(g), rsend.at[4 * dx + dy], rrecv.at[4 * dx + dy], mate)
    for cp in own:
        cp.wait()
    for d in order:
        remote(cbuf.at[(z - d + 8) % 8], cbuf.at[(z - d + 8) % 8], csend.at[d], crecv.at[d], me, z).wait_recv()
    scp = pltpu.make_async_copy(cbuf, csm, lsem.at[3])
    scp.start()
    for dx in range(4):
        for dy in range(4):
            g = cls_of(x - dx + 4, y - dy + 4, 1 - core)
            k = 4 * dx + dy
            remote(slab(g), slab(g), rsend.at[k], rrecv.at[k], me, z).wait_recv()
    scp.wait()
    c_back = pltpu.make_async_copy(cbuf, cand_out.at[core], lsem.at[0])
    c_back.start()
    c_mate = remote(cbuf, cand_out.at[core], xsend.at[8], xrecv.at[8], mate, z)
    c_mate.start()

    @pl.loop(0, 64)
    def _(b):
        vs = []
        for i in range(8):
            r = rbuf[b * 8 + i].astype(F32)
            s = jnp.sum(r * r, axis=0)
            s = s[:, :HARM] + s[:, HARM:]
            vs.append(s[:, :128] + s[:, 128:])
        norms[pl.ds(pl.multiple_of(b * 8, 8), 8), :] = row_sums(vs)

    @pl.loop(0, 8)
    def _(t):
        d = (t % 2) * ((t + 1) // 2) + (1 - t % 2) * ((8 - t // 2) % 8)
        src = (z - d + 8) % 8

        @pl.when(t > 0)
        def _():
            remote(pbuf.at[src], pbuf.at[src], psend.at[d], precv.at[d], me, z).wait_recv()

        @pl.loop(0, 16)
        def _(i):
            p = pbuf[src, i].astype(F32)
            p_re, p_im = p[:, :, :HARM], p[:, :, HARM:]
            for j0 in (0, 8):
                re, im = [], []
                row = pl.multiple_of(i * CANDS + j0, 8)
                for j in range(8):
                    c = csm[src, (i * CANDS + j0 + j) // 128, (i * CANDS + j0 + j) % 128]
                    r = rbuf[c].astype(F32)
                    r_re, r_im = r[:, :, :HARM], r[:, :, HARM:]
                    re.append(jnp.sum(p_re * r_re + p_im * r_im, axis=0))
                    im.append(jnp.sum(p_im * r_re - p_re * r_im, axis=0))
                    normrow[pl.ds(i * CANDS + j0 + j, 1), :] = norms[pl.ds(c, 1), :]
                cross[pl.ds(row, 8), :HARM] = row_sums(re)
                cross[pl.ds(row, 8), HARM:WIDTH] = row_sums(im)

        cross[:, WIDTH:] = normrow[...]
        total = jnp.zeros((ANG, 256), F32)
        for part3 in parts3(cross[...]):
            out = lax.dot_general(
                fwd[...], part3, (((1,), (1,)), ((), ())), preferred_element_type=F32
            )
            total = total + (out[:ANG] + (out[ANG : 2 * ANG] + out[2 * ANG : 3 * ANG]))
        cout[d] = total

        @pl.when(t > 0)
        def _():
            remote(cout.at[d], cin.at[d], csem_s.at[d], csem_r.at[d], me, src).start()

    halves_cp = pltpu.make_async_copy(pbuf.at[:, :, core], halves.at[core], lsem.at[2])
    halves_cp.start()
    halves_mate = remote(pbuf.at[:, :, 1 - core], halves.at[core], xsend.at[9], xrecv.at[9], mate, z)
    halves_mate.start()
    corr = cout[0]
    for d in range(1, 8):
        remote(cin.at[d], cin.at[d], csem_s.at[d], csem_r.at[d], me, z).wait_recv()
        corr = corr + cin[d]
    angle = lax.broadcasted_iota(jnp.int32, (ANG, 128), 0)
    for lanes in (slice(0, 128), slice(128, 256)):
        score = jnp.where(angle < ROTS, corr[:, lanes] * SCALE, -1e30)
        top = group_all(jnp.broadcast_to(jnp.max(score, axis=0, keepdims=True), (8, 128)), jnp.maximum)
        expo = jnp.where(angle < ROTS, jnp.exp(score - top[:1]), 0.0)
        den = group_all(jnp.broadcast_to(jnp.sum(expo, axis=0, keepdims=True), (8, 128)), jnp.add)
        lse = top + jnp.log(den)
        lse_out[:, lanes] = lse
        wown[:, lanes] = jnp.where(angle < ROTS, jnp.exp(score - lse[:1]), 0.0)
    w_cp = [
        remote(wown, weights.at[core, z], wsend.at[d], wrecv.at[d], me, (z + d) % 8) for d in order
    ]
    w_cp.append(remote(wown, weights.at[core, z], xsend.at[0], xrecv.at[0], mate, z))
    for cp in w_cp:
        cp.start()
    w_own = pltpu.make_async_copy(wown, weights.at[core, z], lsem.at[1])
    w_own.start()
    for d in order:
        land = weights.at[core, (z - d + 8) % 8]
        remote(land, land, wsend.at[d], wrecv.at[d], me, z).wait_recv()
        pass_on(land, xsend.at[d], xrecv.at[d], mate)

    for d in range(8):
        land = weights.at[1 - core, (z - d + 8) % 8]
        remote(land, land, xsend.at[d], xrecv.at[d], me, z).wait_recv()
    remote(cbuf, cand_out.at[1 - core], xsend.at[8], xrecv.at[8], me, z).wait_recv()
    remote(pbuf.at[:, :, core], halves.at[1 - core], xsend.at[9], xrecv.at[9], me, z).wait_recv()
    for cp in (w_own, c_back, halves_cp):
        cp.wait()
    for cp in c_cp + r_cp + p_cp + sent + [c_mate, halves_mate] + w_cp:
        cp.wait_send()
    for d in range(1, 8):
        remote(cout.at[d], cin.at[d], csem_s.at[d], csem_r.at[d], me, z).wait_send()


def sums_kernel(cand, halves, w_ref, bwd, out_ref, tot_ref, mixed, acc, accw):
    @pl.loop(0, 16)
    def _(b):
        w = w_ref[b // 8, b % 8]
        high, mid, low = [v.astype(F32) for v in parts3(w)]
        lhs = jnp.concatenate([high, mid, low, high, mid, high], 0).astype(BF16)
        y = lax.dot_general(
            lhs, bwd[...], (((0,), (0,)), ((), ())), preferred_element_type=F32
        )
        rows = pl.ds(pl.multiple_of(b * 256, 256), 256)
        mixed[rows, :WIDTH] = y[:, :WIDTH].astype(BF16).astype(F32)
        mixed[rows, WIDTH:] = y[:, WIDTH:]

    @pl.loop(0, acc.shape[0] // 8)
    def _(c):
        acc[pl.ds(c * 8, 8)] = jnp.zeros((8, 8, WIDTH), F32)

    accw[...] = jnp.zeros_like(accw)

    @pl.loop(0, 256)
    def _(n):
        p = halves[n // 128, (n // 16) % 8, n % 16].astype(F32)
        p_re, p_im = p[:, :HARM], p[:, HARM:]
        for j0 in range(0, CANDS, 4):
            cs, new, neww = [], [], []
            for j in range(4):
                pair = n * CANDS + j0 + j
                c = cand[n // 128, (n // 16) % 8, (pair // 128) % 2, pair % 128]
                row = mixed[pl.ds(pair, 1), :]
                y_re, y_im = row[:, :HARM], row[:, HARM:WIDTH]
                cs.append(c)
                new.append(
                    (
                        acc[c, :, :HARM] + (p_re * y_re - p_im * y_im),
                        acc[c, :, HARM:] + (p_re * y_im + p_im * y_re),
                    )
                )
                neww.append(accw[pl.ds(c, 1), :] + row[:, WIDTH:])
            for c, (re, im), tot in zip(cs, new, neww):
                acc[c, :, :HARM] = re
                acc[c, :, HARM:] = im
                accw[pl.ds(c, 1), :] = tot

    @pl.loop(0, acc.shape[0] // 8)
    def _(c):
        out_ref[pl.ds(c * 8, 8)] = acc[pl.ds(c * 8, 8)].astype(BF16)

    diag = lax.broadcasted_iota(jnp.int32, (128, 128), 0) == lax.broadcasted_iota(
        jnp.int32, (128, 128), 1
    )
    rows = [
        jnp.sum(jnp.where(diag, accw[128 * b : 128 * b + 128, :], 0.0), axis=0, keepdims=True)
        for b in range(4)
    ]
    tot_ref[...] = jnp.concatenate(rows + [jnp.zeros((4, 128), F32)], 0)


def scatter_kernel(
    part, tot,
    out_ref, tot_out,
    a1, b1, s2, r2, fin, totin,
    lsem, s1send, s1recv, s2send, s2recv, tsend, trecv, xsend, xrecv,
):
    x, y, core, z = where_am_i()
    me = cls_of(x, y, core)
    mate = cls_of(x, y, 1 - core)
    offsets = [(dx, dy) for dx in range(4) for dy in range(4) if dx or dy]
    greet([(cls_of(x + dx, y + dy, core), z) for dx, dy in offsets] + [(mate, z)])
    t_cp = [
        remote(tot, totin.at[4 * dx + dy], tsend.at[4 * dx + dy], trecv.at[4 * dx + dy], cls_of(x + dx, y + dy, core), z)
        for dx, dy in offsets
    ]
    cps = []
    for d in (2, 1, 3):
        cps.append(remote(part.at[(x + d) % 4, :, 0], a1.at[d], s1send.at[0, d], s1recv.at[0, d], cls_of(x + d, y, core), z))
        cps.append(remote(part.at[:, (y + d) % 4, 1], b1.at[d], s1send.at[1, d], s1recv.at[1, d], cls_of(x, y + d, core), z))
    for cp in t_cp + cps:
        cp.start()
    own = [
        pltpu.make_async_copy(part.at[x, :, 0], a1.at[0], lsem.at[0]),
        pltpu.make_async_copy(part.at[:, y, 1], b1.at[0], lsem.at[1]),
    ]
    for cp in own:
        cp.start()
    for cp in own:
        cp.wait()
    for k, land in enumerate((a1, b1)):
        for d in range(1, 4):
            remote(land.at[d], land.at[d], s1send.at[k, d], s1recv.at[k, d], me, z).wait_recv()
        mine = (y, x)[k]
        for d in (2, 1, 3, 0):
            to = (mine + d) % 4

            @pl.loop(0, 16)
            def _(q, d=d, to=to, land=land, k=k):
                total = (land[0, to, q].astype(F32) + land[1, to, q].astype(F32)) + (
                    land[2, to, q].astype(F32) + land[3, to, q].astype(F32)
                )
                if d:
                    s2[k, d, q] = total.astype(BF16)
                else:
                    fin[k, q] = total

            if d:
                dest = (cls_of(x, y + d, core), cls_of(x + d, y, core))[k]
                cp = remote(s2.at[k, d], r2.at[k, d], s2send.at[k, d], s2recv.at[k, d], dest, z)
                cp.start()
                cps.append(cp)
    for k in range(2):
        for d in range(1, 4):
            remote(r2.at[k, d], r2.at[k, d], s2send.at[k, d], s2recv.at[k, d], me, z).wait_recv()

        @pl.loop(0, 16)
        def _(q, k=k):
            fin[k, q] = fin[k, q] + (
                (r2[k, 1, q].astype(F32) + r2[k, 2, q].astype(F32)) + r2[k, 3, q].astype(F32)
            )

    cross_cp = remote(fin.at[1 - core], out_ref.at[:, core], xsend.at[0], xrecv.at[0], mate, z)
    cross_cp.start()
    keep = pltpu.make_async_copy(fin.at[core], out_ref.at[:, core], lsem.at[0])
    keep.start()
    total = tot[...]
    for dx, dy in offsets:
        k = 4 * dx + dy
        remote(totin.at[k], totin.at[k], tsend.at[k], trecv.at[k], me, z).wait_recv()
        total = total + totin[k]
    tot_out[...] = total
    remote(fin.at[core], out_ref.at[:, 1 - core], xsend.at[0], xrecv.at[0], me, z).wait_recv()
    keep.wait()
    for cp in t_cp + cps + [cross_cp]:
        cp.wait_send()


def spec(space):
    return pl.BlockSpec(memory_space=space)


def sds(shape, dtype):
    return jax.ShapeDtypeStruct(shape, dtype)


def per_device(particles, references, owner_groups, class_order):
    count = particles.shape[0]
    groups = references.shape[0]
    core = lax.axis_index("cls") % 2
    place = lax.axis_index("cls") % 8 // 2 * 32 + core * 16
    fwd, bwd = spectral_tables()
    own_cand = (owner_groups[:, :, None] * groups + class_order[:, :, :CAND_OWN]).reshape(2, 128)

    halves, weights, cand, lse = pl.pallas_call(
        assign_kernel,
        out_shape=(
            sds((2, 8, 16, 8, WIDTH), BF16),
            sds((2, 8, ANG, 256), F32),
            sds((2, 8, 2, 128), jnp.int32),
            sds((8, 256), F32),
        ),
        in_specs=[spec(ANY), spec(ANY), spec(VMEM), spec(VMEM)],
        out_specs=[spec(ANY), spec(ANY), spec(ANY), spec(VMEM)],
        scratch_shapes=[
            VMEM((8, 16, 2, 8, WIDTH), BF16),
            VMEM((512, 2, 8, WIDTH), BF16),
            VMEM((8, 2, 128), jnp.int32),
            SMEM((8, 2, 128), jnp.int32),
            VMEM((256, EXT), F32),
            VMEM((256, 128), F32),
            VMEM((512, 128), F32),
            VMEM((8, ANG, 256), F32),
            VMEM((8, ANG, 256), F32),
            VMEM((ANG, 256), F32),
            DMA((4,)), DMA((8,)), DMA((8,)), DMA((8,)), DMA((8,)), DMA((6,)), DMA((6,)),
            DMA((2, 9)), DMA((2, 9)), DMA((16,)), DMA((16,)), DMA((8,)), DMA((8,)),
            DMA((8,)), DMA((8,)), DMA((10,)), DMA((10,)),
        ],
        compiler_params=pltpu.CompilerParams(
            collective_id=0, has_side_effects=True, vmem_limit_bytes=48 * 2**20
        ),
    )(
        particles.reshape(count, 8, 2, 8, WIDTH),
        references.reshape(groups, 8, 2, 8, WIDTH),
        own_cand,
        fwd,
    )
    sums, totals = pl.pallas_call(
        sums_kernel,
        out_shape=(sds((512, 8, WIDTH), BF16), sds((8, 128), F32)),
        in_specs=[spec(SMEM), spec(VMEM), spec(VMEM), spec(VMEM)],
        out_specs=[spec(VMEM), spec(VMEM)],
        scratch_shapes=[
            VMEM((4096, EXT), F32),
            VMEM((512, 8, WIDTH), F32),
            VMEM((512, 128), F32),
        ],
        compiler_params=pltpu.CompilerParams(vmem_limit_bytes=56 * 2**20),
    )(cand, halves, weights, bwd)
    class_sums, class_tot = pl.pallas_call(
        scatter_kernel,
        out_shape=(sds((16, 2, 8, WIDTH), F32), sds((8, 128), F32)),
        in_specs=[spec(ANY), spec(VMEM)],
        out_specs=[spec(VMEM), spec(VMEM)],
        scratch_shapes=[
            VMEM((4, 4, 16, 8, WIDTH), BF16),
            VMEM((4, 4, 16, 8, WIDTH), BF16),
            VMEM((2, 4, 16, 8, WIDTH), BF16),
            VMEM((2, 4, 16, 8, WIDTH), BF16),
            VMEM((2, 16, 8, WIDTH), F32),
            VMEM((16, 8, 128), F32),
            DMA((2,)), DMA((2, 4)), DMA((2, 4)), DMA((2, 4)), DMA((2, 4)),
            DMA((16,)), DMA((16,)), DMA((1,)), DMA((1,)),
        ],
        compiler_params=pltpu.CompilerParams(
            collective_id=1, has_side_effects=True, vmem_limit_bytes=48 * 2**20
        ),
    )(sums.reshape(4, 4, 2, 16, 8, WIDTH), totals)
    row = lax.dynamic_index_in_dim(class_tot, lax.axis_index("cls") // 8, 0, keepdims=False)
    class_weights = lax.dynamic_slice_in_dim(row, place, 16)
    log_norm = lse[0].reshape(count, CANDS)[:, 0]
    return (class_sums.reshape(groups, 16, WIDTH), class_weights, log_norm)


def solution(mesh):
    in_specs = (
        P(("cls", "prt"), None, None),
        P("cls", None, None),
        P(("cls", "prt"), None),
        P(("cls", "prt"), None, None),
    )
    out_specs = (P("cls", "prt", None), P("cls"), P(("cls", "prt")))
    return jax.shard_map(
        per_device, mesh=mesh, in_specs=in_specs, out_specs=out_specs, check_vma=False
    )
```

time: 346 us -> 204 us (0.59)
  blocking collectives: 150 us -> 0 us
  Pallas kernels: 66.2 us -> 191 us
  waiting for transfers between devices: 91 us -> 0 us
  between operations: 14.5 us -> 0.74 us
  starting transfers between devices: 9.25 us -> 0 us
    pallas_call x2 -> x3, Pallas kernels: 66.2 us -> 191 us  [the longest x1 88.5 us: per_device(): pl.pallas_call(assign_kernel, out_shape=(sds((2, 8, 16, 8, WIDTH), BF16),...]
    reduce_scatter x2 -> x0, waiting for transfers between devices: 90.9 us -> none  [the longest x1 54.8 us: per_device(): class_sums = lax.psum_scatter(sums, 'cls', scatter_dimension=0, tiled=True)]
    all_gather x2 -> x0, blocking collectives: 76.1 us -> none  [the longest x1 55 us: per_device(): cand = lax.all_gather(own_cand, 'prt', axis=0, tiled=True)]
    unnamed x1 -> x0, blocking collectives: 73.4 us -> none
    all_to_all x1 -> x0, starting transfers between devices: 9.13 us -> none  [per_device(): lax.all_to_all(particles.reshape(count, n_prt, depth, width), 'prt', spli...]
    unnamed x16, local copies, waits for them, and re-layouts: 3.61 us -> 9.53 us
  transfers between devices with their start and end apart: 4 -> 0, of which waited for: 2 -> 0; matrix products, arithmetic and copies ran while one was open for 2% -> 0% of each run, Pallas kernels for 0% -> 0%
where the time goes in v2:
time: 204 us
  Pallas kernels  191 us (94%)
  local copies, waits for them, and re-layouts  10.4 us (5%)
    pallas_call x1, Pallas kernels, per_device(): pl.pallas_call(assign_kernel, out_shape=(sds((2, 8, 16, 8, WIDTH), BF16),...  88.5 us
    pallas_call x1, Pallas kernels, per_device(): pl.pallas_call(sums_kernel, out_shape=(sds((512, 8, WIDTH), BF16), sds((8...  64.2 us
    pallas_call x1, Pallas kernels, per_device(): pl.pallas_call(scatter_kernel, out_shape=(sds((16, 2, 8, WIDTH), F32), sd...  38.7 us
    unnamed x16, local copies, waits for them, and re-layouts  9.53 us

profile of v2, /device:TPU:1, one launch (start us, length us, event | category | flops | bytes accessed | tf_op | source)
XLA Modules:
  0.0 204.1 jit_solution(11431393793858168621)
XLA Ops:
  0.7 0.7 broadcast_multiply_fusion
  1.4 0.1 copy.11
  1.5 0.8 slice_add_fusion
  2.3 0.1 reshape.26.cand
  2.4 0.0 copy-start.1
  2.4 1.6 copy-done.1
  4.0 0.0 copy-start.4
  4.0 0.9 copy-done.4
  4.9 88.5 %shard_map.85 = (bf16[2,8,16,8,512]{4,3,2,1,0:T(8,128)(2,1)S(1)}, f32[2,8,40,256]{3,2,1,0:T(8,128)S(1)}, s32[2,8,2,128]{3,2,1,0:T(2,128)S(1)}, f32[8,256]{1,0:T(8,128)S(1)}) custom-call(bf16[16,8,2,8,512]{4,3,2,1,0:T(8,128)(2,1)S(1)} %bitcast.9, bf16[16,8,2,8,512]{4,3,2,1,0:T(8,128)(2,1)} %bitcast.11, s32[2,128]{1,0:T(2,128)S(1)} %reshape.26.cand, ...), custom_call_target="tpu_custom_call" | custom-call | tf_op jit(solution)/shard_map/pallas_call | solution.py:436
  93.5 0.0 copy-start.2
  93.5 1.3 copy-done.2
  94.8 0.0 copy-start.3
  94.8 0.8 copy-done.3
  95.6 0.0 copy-start.5
  95.6 0.6 copy-done.5
  96.3 0.1 reshape_squeeze.3
  96.3 0.6 copy.13
  96.9 64.2 %shard_map.86 = (bf16[512,8,512]{2,1,0:T(8,128)(2,1)}, f32[8,128]{1,0:T(8,128)}) custom-call(s32[2,8,2,128]{3,2,1,0:T(2,128)} %copy-done.5, bf16[2,8,16,8,512]{4,3,2,1,0:T(8,128)(2,1)} %copy-done.2, f32[2,8,40,256]{3,2,1,0:T(8,128)} %copy-done.3, bf16[240,640]{1,0:T(8,128)(2,1)} %constant.78.clone.bwd), custom_call_target="tpu_custom_call" | custom-call | tf_op jit(solution)/shard_map/pallas_call | solution.py:470
  161.1 0.0 copy-start
  161.1 2.2 %copy-done = bf16[512,8,512]{2,1,0:T(8,128)(2,1)S(1)} copy-done((bf16[512,8,512]{2,1,0:T(8,128)(2,1)S(1)}, bf16[512,8,512]{2,1,0:T(8,128)(2,1)}, u32[]{:S(2)}) %copy-start) | copy-done | bytes 4194328
  163.3 0.7 copy-done.6
  164.0 38.7 %shard_map.87 = (f32[16,2,8,512]{3,2,1,0:T(8,128)S(1)}, f32[8,128]{1,0:T(8,128)S(1)}) custom-call(bf16[4,4,2,16,8,512]{5,4,3,2,1,0:T(8,128)(2,1)S(1)} %bitcast.8, f32[8,128]{1,0:T(8,128)S(1)} %copy-done.6), custom_call_target="tpu_custom_call" | custom-call | tf_op jit(solution)/shard_map/pallas_call | solution.py:482
  202.7 0.6 dynamic-slice_bitcast_fusion
  203.3 0.8 copy.15
  (2 shorter events, 0.0 us)
Async XLA Ops:
  2.4 1.6 copy-start.1
  4.0 0.9 copy-start.4
  93.5 1.3 copy-start.2
  94.8 0.8 copy-start.3
  95.6 0.6 copy-start.5
  161.1 2.2 %copy-start = (bf16[512,8,512]{2,1,0:T(8,128)(2,1)S(1)}, bf16[512,8,512]{2,1,0:T(8,128)(2,1)}, u32[]{:S(2)}) copy-start(bf16[512,8,512]{2,1,0:T(8,128)(2,1)} %get-tuple-element.14) | copy-start | bytes 12582916
  163.3 0.7 copy-start.6

commit v3 on v2

v3 whole, which is shorter than its diff:
```python
import functools
import math

import jax
import jax.numpy as jnp
import numpy as np
from jax import lax
from jax.experimental import pallas as pl
from jax.experimental.pallas import tpu as pltpu
from jax.sharding import PartitionSpec as P

CYCLES = 128
HARM = 256
WIDTH = 2 * HARM
ROTS = 36
OWN_TOP = 4
CAND_OWN = 4
CANDS = OWN_TOP * CAND_OWN
ANG = 40
EXT = WIDTH + 128
VMEM, SMEM, ANY = pltpu.VMEM, pltpu.SMEM, pl.ANY
F32, BF16 = jnp.float32, jnp.bfloat16
DMA = pltpu.SemaphoreType.DMA
SCALE = 2.0 / math.sqrt(CYCLES * WIDTH)


def split3(x):
    high = x.astype(jnp.bfloat16).astype(np.float32)
    mid = (x - high).astype(jnp.bfloat16).astype(np.float32)
    low = (x - high - mid).astype(jnp.bfloat16).astype(np.float32)
    return high, mid, low


def spectral_tables():
    harmonic = np.arange(HARM, dtype=np.float32)
    angles = np.float32(2.0 * math.pi) * np.arange(ROTS, dtype=np.float32) / np.float32(ROTS)
    phase = (harmonic[:, None] * angles[None, :]).astype(np.float64)
    cos, sin = np.cos(phase).astype(np.float32).T, np.sin(phase).astype(np.float32).T
    forward = np.zeros((ANG, EXT), np.float32)
    forward[:ROTS, :HARM], forward[:ROTS, HARM:WIDTH] = cos, sin
    forward[:ROTS, WIDTH:] = -0.5
    backward = np.zeros((ANG, EXT), np.float32)
    backward[:ROTS, :HARM], backward[:ROTS, HARM:WIDTH] = cos, -sin
    backward[:ROTS, WIDTH:] = 1.0
    f_high, f_mid, f_low = split3(forward)
    b_high, b_mid, b_low = split3(backward)
    fwd = np.concatenate([f_high, f_mid, f_low, np.zeros((8, EXT), np.float32)], 0)
    bwd = np.concatenate([b_high, b_high, b_high, b_mid, b_mid, b_low], 0)
    return jnp.asarray(fwd, BF16), jnp.asarray(bwd, BF16)


def parts3(x):
    high = x.astype(BF16)
    rest = x - high.astype(F32)
    mid = rest.astype(BF16)
    low = (rest - mid.astype(F32)).astype(BF16)
    return high, mid, low


def row_sums(vs):
    row = lax.broadcasted_iota(jnp.int32, vs[0].shape, 0)
    for step in (1, 2, 4):
        keep = (row % (2 * step)) < step
        vs = [
            jnp.where(keep, a, b) + pltpu.roll(jnp.where(keep, b, a), 8 - step, 0)
            for a, b in zip(vs[0::2], vs[1::2])
        ]
    return vs[0]


def group_all(x, op):
    lane = lax.broadcasted_iota(jnp.int32, x.shape, 1)
    n = x.shape[1]
    for step in (1, 2, 4, 8):
        other = jnp.where(
            (lane // step) % 2 == 0, pltpu.roll(x, n - step, 1), pltpu.roll(x, step, 1)
        )
        x = op(x, other)
    return x


def where_am_i():
    cls = lax.axis_index("cls")
    return cls // 8, (cls // 2) % 4, cls % 2, lax.axis_index("prt")


def cls_of(x, y, core):
    return (x % 4) * 8 + (y % 4) * 2 + core


def remote(src, dst, send, recv, cls, prt):
    return pltpu.make_async_remote_copy(
        src, dst, send, recv, device_id=(cls, prt), device_id_type=pl.DeviceIdType.MESH
    )


def greet(peers):
    barrier = pltpu.get_barrier_semaphore()
    for cls, prt in peers:
        pl.semaphore_signal(
            barrier, inc=1, device_id=(cls, prt), device_id_type=pl.DeviceIdType.MESH
        )
    pl.semaphore_wait(barrier, len(peers))


def assign_kernel(
    part, refs, cand, fwd_hbm,
    halves, weights, cand_out, lse_out,
    pbuf, rbuf, rcomb, cbuf, csm, cross, normrow, norms, cout, cin, wown, fwd, lsem, ssem, rsem,
):
    x, y, core, z = where_am_i()
    me = cls_of(x, y, core)
    mate = cls_of(x, y, 1 - core)
    greet(
        [(me, (z + d) % 8) for d in range(1, 8)]
        + [(cls_of(x + d, y, core), z) for d in (1, 3)]
        + [(cls_of(x, y + d, core), z) for d in (1, 3)]
        + [(mate, z)]
    )
    around = (1, 7, 2, 6, 3, 5, 4)

    def at(dx, dy, col=None):
        return cls_of(x - dx + 4, y - dy + 4, core if col is None else col)

    def go(dx, dy):
        return cls_of(x + dx + 4, y + dy + 4, core)

    def piece(g, start=0, size=16):
        return rbuf.at[pl.ds(g * 16 + start, size)]

    sent = []

    def send(src, dst, k, cls, prt):
        cp = remote(src, dst, ssem.at[k], rsem.at[k], cls, prt)
        cp.start()
        sent.append(cp)

    def pass_on(ref, k, cls):
        send(ref, ref, k, cls, z)

    def arrive(ref, k):
        remote(ref, ref, ssem.at[k], rsem.at[k], me, z).wait_recv()

    for d in around:
        send(cand, cbuf.at[z], d, me, (z + d) % 8)
    own_refs = refs.at[:, z]
    for k, dx, dy in ((16, 1, 0), (17, -1, 0), (18, 0, 1), (19, 0, -1)):
        send(own_refs, piece(me), k, go(dx, dy), z)
    send(own_refs, piece(me), 64, mate, z)
    for d in around:
        send(part.at[:, (z + d) % 8], pbuf.at[z], 80 + d, me, (z + d) % 8)
    own = [
        pltpu.make_async_copy(cand, cbuf.at[z], lsem.at[0]),
        pltpu.make_async_copy(own_refs, piece(me), lsem.at[1]),
        pltpu.make_async_copy(part.at[:, z], pbuf.at[z], lsem.at[2]),
    ]
    fwd_cp = pltpu.make_async_copy(fwd_hbm, fwd, lsem.at[4])
    for cp in own + [fwd_cp]:
        cp.start()

    def to_mate(dx, dy):
        pass_on(piece(at(dx, dy)), 64 + 4 * dx + dy, mate)

    for k, (dx, dy) in ((16, (1, 0)), (18, (0, 1)), (17, (3, 0)), (19, (0, 3))):
        g = at(dx, dy)
        arrive(piece(g), k)
        if dy == 0:
            pass_on(piece(g, 0 if dx == 1 else 8, 8), 20 + (dx == 3), go(2 - dx, 0))
            pass_on(piece(g, 0, 8), 24 + 2 * (dx - 1), go(0, 1))
            pass_on(piece(g, 0, 8), 25 + 2 * (dx - 1), go(0, -1))
        else:
            pass_on(piece(g, 0 if dy == 1 else 8, 8), 22 + (dy == 3), go(0, 2 - dy))
            pass_on(piece(g, 8, 8), 30 + 2 * (dy - 1), go(1, 0))
            pass_on(piece(g, 8, 8), 31 + 2 * (dy - 1), go(-1, 0))
        to_mate(dx, dy)
    g = at(2, 0)
    arrive(piece(g, 0, 8), 20)
    pass_on(piece(g, 0, 8), 26, go(0, 1))
    pass_on(piece(g, 0, 8), 27, go(0, -1))
    g = at(0, 2)
    arrive(piece(g, 8, 8), 23)
    pass_on(piece(g, 8, 8), 32, go(1, 0))
    pass_on(piece(g, 8, 8), 33, go(-1, 0))
    for m in (1, 3, 2):
        for side in range(2):
            dy = 1 + 2 * side
            g = at(m, dy)
            arrive(piece(g, 0, 8), 24 + 2 * (m - 1) + side)
            pass_on(piece(g, 4 * side, 4), 36 + 2 * (m - 1) + side, go(0, 1 - 2 * side))
            g = at(dy, m)
            arrive(piece(g, 8, 8), 30 + 2 * (m - 1) + side)
            pass_on(piece(g, 8 + 4 * side, 4), 42 + 2 * (m - 1) + side, go(1 - 2 * side, 0))
    arrive(piece(at(2, 0), 8, 8), 21)
    to_mate(2, 0)
    arrive(piece(at(0, 2), 0, 8), 22)
    to_mate(0, 2)
    for dx in (1, 3):
        for dy in (1, 3):
            to_mate(dx, dy)
    for m in (1, 3, 2):
        for side in range(2):
            arrive(piece(at(m, 2), 4 * side, 4), 36 + 2 * (m - 1) + side)
            arrive(piece(at(2, m), 8 + 4 * side, 4), 42 + 2 * (m - 1) + side)
        to_mate(m, 2)
        if m != 2:
            to_mate(2, m)
    for cp in own:
        cp.wait()
    for d in around:
        arrive(cbuf.at[(z - d + 8) % 8], d)
    scp = pltpu.make_async_copy(cbuf, csm, lsem.at[3])
    scp.start()
    c_back = pltpu.make_async_copy(cbuf, cand_out.at[core], lsem.at[0])
    c_back.start()
    send(cbuf, cand_out.at[core], 12, mate, z)

    def norms_of(g):
        @pl.loop(0, 2)
        def _(b):
            vs = []
            for i in range(8):
                k = g * 16 + b * 8 + i
                r = rbuf[k].astype(F32)
                re, im = r[:, :, :HARM], r[:, :, HARM:]
                rcomb[k, 0] = re
                rcomb[k, 1] = re + im
                rcomb[k, 2] = im - re
                s = jnp.sum(re * re + im * im, axis=0)
                vs.append(s[:, :128] + s[:, 128:])
            norms[pl.ds(pl.multiple_of(g * 16 + b * 8, 8), 8), :] = row_sums(vs)

    slices = [(0, 0), (1, 0), (0, 1), (3, 0), (0, 3), (2, 0), (0, 2), (1, 1), (1, 3), (3, 1), (3, 3)]
    slices += [(1, 2), (2, 1), (3, 2), (2, 3), (2, 2)]

    @pl.loop(0, 16)
    def _(k):
        norms_of(2 * k + core)

    for dx, dy in slices:
        arrive(piece(at(dx, dy, 1 - core)), 64 + 4 * dx + dy)

    @pl.loop(0, 16)
    def _(k):
        norms_of(2 * k + 1 - core)

    scp.wait()
    fwd_cp.wait()

    @pl.loop(0, 8)
    def _(t):
        d = (t % 2) * ((t + 1) // 2) + (1 - t % 2) * ((8 - t // 2) % 8)
        src = (z - d + 8) % 8

        @pl.when(t > 0)
        def _():
            arrive(pbuf.at[src], 80 + d)

        @pl.loop(0, 2)
        def _(hi):
            @pl.loop(0, 8)
            def _(lo):
                i = hi * 8 + lo
                p = pbuf[src, i].astype(F32)
                p_re, p_im = p[:, :, :HARM], p[:, :, HARM:]
                p_sum = p_re + p_im
                for j0 in (0, 8):
                    re, im = [], []
                    row = pl.multiple_of(i * CANDS + j0, 8)
                    for j in range(8):
                        c = csm[src, hi, lo * CANDS + (j0 + j)]
                        k1 = jnp.sum(p_sum * rcomb[c, 0], axis=0)
                        k2 = jnp.sum(p_re * rcomb[c, 1], axis=0)
                        k3 = jnp.sum(p_im * rcomb[c, 2], axis=0)
                        re.append(k1 + k3)
                        im.append(k1 - k2)
                        normrow[pl.ds(i * CANDS + j0 + j, 1), :] = norms[pl.ds(c, 1), :]
                    cross[pl.ds(row, 8), :HARM] = row_sums(re)
                    cross[pl.ds(row, 8), HARM:WIDTH] = row_sums(im)

        cross[:, WIDTH:] = normrow[...]
        total = jnp.zeros((ANG, 256), F32)
        for part3 in parts3(cross[...]):
            out = lax.dot_general(
                fwd[...], part3, (((1,), (1,)), ((), ())), preferred_element_type=F32
            )
            total = total + (out[:ANG] + (out[ANG : 2 * ANG] + out[2 * ANG : 3 * ANG]))
        cout[d] = total

        @pl.when(t > 0)
        def _():
            remote(cout.at[d], cin.at[d], ssem.at[88 + d], rsem.at[88 + d], me, src).start()

    halves_cp = pltpu.make_async_copy(pbuf.at[:, :, core], halves.at[core], lsem.at[2])
    halves_cp.start()
    send(pbuf.at[:, :, 1 - core], halves.at[core], 13, mate, z)
    corr = cout[0]
    for d in range(1, 8):
        arrive(cin.at[d], 88 + d)
        corr = corr + cin[d]
    angle = lax.broadcasted_iota(jnp.int32, (ANG, 128), 0)
    for lanes in (slice(0, 128), slice(128, 256)):
        score = jnp.where(angle < ROTS, corr[:, lanes] * SCALE, -1e30)
        top = group_all(jnp.broadcast_to(jnp.max(score, axis=0, keepdims=True), (8, 128)), jnp.maximum)
        expo = jnp.where(angle < ROTS, jnp.exp(score - top[:1]), 0.0)
        den = group_all(jnp.broadcast_to(jnp.sum(expo, axis=0, keepdims=True), (8, 128)), jnp.add)
        lse = top + jnp.log(den)
        lse_out[:, lanes] = lse
        wown[:, lanes] = jnp.where(angle < ROTS, jnp.exp(score - lse[:1]), 0.0)
    for d in around:
        send(wown, weights.at[core, z], 96 + d, me, (z + d) % 8)
    send(wown, weights.at[core, z], 104, mate, z)
    w_own = pltpu.make_async_copy(wown, weights.at[core, z], lsem.at[1])
    w_own.start()
    for d in (1, 7, 2, 6, 3, 5, 4):
        land = weights.at[core, (z - d + 8) % 8]
        arrive(land, 96 + d)
        pass_on(land, 104 + d, mate)

    for d in range(8):
        arrive(weights.at[1 - core, (z - d + 8) % 8], 104 + d)
    arrive(cand_out.at[1 - core], 12)
    arrive(halves.at[1 - core], 13)
    for cp in (w_own, c_back, halves_cp):
        cp.wait()
    for cp in sent:
        cp.wait_send()
    for d in range(1, 8):
        remote(cout.at[d], cin.at[d], ssem.at[88 + d], rsem.at[88 + d], me, z).wait_send()


def sums_kernel(
    cand, halves_hbm, w_hbm, bwd_hbm,
    out_ref, own_ref, tot_ref,
    halves, w_ref, bwd, mixed, tots, acc, accw, obuf, lsem, osem,
):
    x, y, _, _ = where_am_i()
    loads = [
        pltpu.make_async_copy(w_hbm, w_ref, lsem.at[0]),
        pltpu.make_async_copy(bwd_hbm, bwd, lsem.at[1]),
        pltpu.make_async_copy(halves_hbm, halves, lsem.at[2]),
    ]
    for cp in loads:
        cp.start()

    @pl.loop(0, acc.shape[0] // 8)
    def _(c):
        acc[pl.ds(c * 8, 8)] = jnp.zeros((8, 8, WIDTH), F32)

    accw[...] = jnp.zeros_like(accw)
    loads[0].wait()
    loads[1].wait()

    @pl.loop(0, 16)
    def _(b):
        w = w_ref[b // 8, b % 8]
        high, mid, low = [v.astype(F32) for v in parts3(w)]
        lhs = jnp.concatenate([high, mid, low, high, mid, high], 0).astype(BF16)
        y = lax.dot_general(
            lhs, bwd[...], (((0,), (0,)), ((), ())), preferred_element_type=F32
        )
        block = pl.ds(b * 16, 16)
        mixed[block] = y[:, :WIDTH].astype(BF16).astype(F32).reshape(16, CANDS, WIDTH)
        tots[block] = y[:, WIDTH:].reshape(16, CANDS, 128)

    loads[2].wait()

    @pl.loop(0, 32)
    def _(b):
        @pl.loop(0, 8)
        def _(lo):
            p = halves[b * 8 + lo].astype(F32)
            p_re, p_im = p[:, :HARM], p[:, HARM:]
            for j0 in range(0, CANDS, 8):
                cs, new, neww = [], [], []
                for j in range(j0, j0 + 8):
                    c = cand[b, lo * CANDS + j]
                    row = mixed[b * 8 + lo, pl.ds(j, 1), :]
                    y_re, y_im = row[:, :HARM], row[:, HARM:]
                    cs.append(c)
                    new.append(
                        (
                            acc[c, :, :HARM] + (p_re * y_re - p_im * y_im),
                            acc[c, :, HARM:] + (p_re * y_im + p_im * y_re),
                        )
                    )
                    neww.append(accw[pl.ds(c, 1), :] + tots[b * 8 + lo, pl.ds(j, 1), :])
                for c, (re, im), tot in zip(cs, new, neww):
                    acc[c, :, :HARM] = re
                    acc[c, :, HARM:] = im
                    accw[pl.ds(c, 1), :] = tot

    out = []
    for k in range(4):
        out.append(pltpu.make_async_copy(acc.at[pl.ds((x * 8 + k * 2) * 16, 16)], own_ref.at[0, k], osem.at[k]))
        out.append(pltpu.make_async_copy(acc.at[pl.ds((k * 8 + y * 2 + 1) * 16, 16)], own_ref.at[1, k], osem.at[4 + k]))
    for cp in out:
        cp.start()
    for k in range(4):

        @pl.loop(0, 16)
        def _(c, k=k):
            at = pl.ds(k * 128 + c * 8, 8)
            obuf[at] = acc[at].astype(BF16)

        at = pl.ds(k * 128, 128)
        out.append(pltpu.make_async_copy(obuf.at[at], out_ref.at[at], osem.at[8 + k]))
        out[-1].start()
    diag = lax.broadcasted_iota(jnp.int32, (128, 128), 0) == lax.broadcasted_iota(
        jnp.int32, (128, 128), 1
    )
    rows = [
        jnp.sum(jnp.where(diag, accw[128 * b : 128 * b + 128, :], 0.0), axis=0, keepdims=True)
        for b in range(4)
    ]
    tot_ref[...] = jnp.concatenate(rows + [jnp.zeros((4, 128), F32)], 0)
    for cp in out:
        cp.wait()


def scatter_kernel(
    part, own_hbm, tot,
    out_ref, tot_out,
    relay, direct, joined, mine, send3, own32, s2, r2, fin, totin,
    lsem, ssem, rsem, tsend, trecv,
):
    x, y, core, z = where_am_i()
    me = cls_of(x, y, core)
    mate = cls_of(x, y, 1 - core)
    offsets = [(dx, dy) for dx in range(4) for dy in range(4) if dx or dy]
    greet([(cls_of(x + dx, y + dy, core), z) for dx, dy in offsets] + [(mate, z)])
    sent = []

    def send(src, dst, k, cls):
        cp = remote(src, dst, ssem.at[k], rsem.at[k], cls, z)
        cp.start()
        sent.append(cp)

    def arrive(ref, k):
        remote(ref, ref, ssem.at[k], rsem.at[k], me, z).wait_recv()

    def sel(k, to, h):
        to = (to + 8) % 4
        return part.at[to, :, 0, h] if k == 0 else part.at[:, to, 1, h]

    def step(k, d, first):
        along_x = (k == 0) == first
        return cls_of(x + d + 4, y, core) if along_x else cls_of(x, y + d + 4, core)

    for dx, dy in offsets:
        k = 4 * dx + dy
        cp = remote(tot, totin.at[k], tsend.at[k], trecv.at[k], cls_of(x + dx, y + dy, core), z)
        cp.start()
        sent.append(cp)
    for k in range(2):
        u = (x, y)[k]
        send(sel(k, u + 2, 0), relay.at[k, 0], 8 * k, step(k, 1, True))
        send(sel(k, u + 2, 1), relay.at[k, 1], 8 * k + 1, step(k, -1, True))
    for k in range(2):
        u = (x, y)[k]
        send(sel(k, u + 1, 1), direct.at[k, 0], 8 * k + 2, step(k, 1, True))
        send(sel(k, u - 1, 0), direct.at[k, 1], 8 * k + 3, step(k, -1, True))
    loads = []
    for k in range(2):
        u = (x, y)[k]
        loads.append(pltpu.make_async_copy(sel(k, u + 1, 0), mine.at[k, 0], lsem.at[3 * k]))
        loads.append(pltpu.make_async_copy(sel(k, u - 1, 1), mine.at[k, 1], lsem.at[3 * k + 1]))
        loads.append(pltpu.make_async_copy(own_hbm.at[k], own32.at[k], lsem.at[3 * k + 2]))
    for cp in loads:
        cp.start()
    for cp in loads:
        cp.wait()
    rounds = (2, 1, 3, 0)
    for k in range(2):
        v = (y, x)[k]
        for side in range(2):
            arrive(relay.at[k, side], 8 * k + side)
        for e in rounds:
            w = (v + e) % 4
            for side in range(2):

                @pl.loop(0, 8)
                def _(q, k=k, w=w, side=side):
                    send3[k, side, w, q] = (
                        relay[k, side, w, q].astype(F32) + mine[k, side, w, q].astype(F32)
                    ).astype(BF16)

                n = 16 + 8 * k + 2 * e + side
                send(send3.at[k, side, w], joined.at[k, side, w], n, step(k, 1 - 2 * side, True))
    for k in range(2):
        for side in range(2):
            arrive(direct.at[k, side], 8 * k + 2 + side)
    for e in rounds:
        for k in range(2):
            v = (y, x)[k]
            w = (v + e) % 4
            for side in range(2):
                arrive(joined.at[k, side, w], 16 + 8 * k + 2 * e + side)

            @pl.loop(0, 8)
            def _(q, k=k, w=w, e=e):
                for side in range(2):
                    total = own32[k, w, side * 8 + q] + (
                        joined[k, side, w, q].astype(F32) + direct[k, 1 - side, w, q].astype(F32)
                    )
                    if e:
                        s2[k, e, side * 8 + q] = total.astype(BF16)
                    else:
                        fin[k, side * 8 + q] = total

            if e:
                send(s2.at[k, e], r2.at[k, e], 32 + 4 * k + e, step(k, e, False))
    for k in range(2):
        for e in (1, 2, 3):
            arrive(r2.at[k, e], 32 + 4 * k + e)

        @pl.loop(0, 16)
        def _(q, k=k):
            fin[k, q] = fin[k, q] + (
                (r2[k, 1, q].astype(F32) + r2[k, 2, q].astype(F32)) + r2[k, 3, q].astype(F32)
            )

    send(fin.at[1 - core], out_ref.at[:, core], 40, mate)
    keep = pltpu.make_async_copy(fin.at[core], out_ref.at[:, core], lsem.at[0])
    keep.start()
    total = tot[...]
    for dx, dy in offsets:
        k = 4 * dx + dy
        remote(totin.at[k], totin.at[k], tsend.at[k], trecv.at[k], me, z).wait_recv()
        total = total + totin[k]
    tot_out[...] = total
    arrive(out_ref.at[:, 1 - core], 40)
    keep.wait()
    for cp in sent:
        cp.wait_send()


def spec(space):
    return pl.BlockSpec(memory_space=space)


def sds(shape, dtype):
    return jax.ShapeDtypeStruct(shape, dtype)


def per_device(particles, references, owner_groups, class_order):
    count = particles.shape[0]
    groups = references.shape[0]
    core = lax.axis_index("cls") % 2
    place = lax.axis_index("cls") % 8 // 2 * 32 + core * 16
    fwd, bwd = spectral_tables()
    own_cand = (owner_groups[:, :, None] * groups + class_order[:, :, :CAND_OWN]).reshape(2, 128)

    halves, weights, cand, lse = pl.pallas_call(
        assign_kernel,
        out_shape=(
            sds((2, 8, 16, 8, WIDTH), BF16),
            sds((2, 8, ANG, 256), F32),
            sds((2, 8, 2, 128), jnp.int32),
            sds((8, 256), F32),
        ),
        in_specs=[spec(ANY), spec(ANY), spec(VMEM), spec(ANY)],
        out_specs=[spec(ANY), spec(ANY), spec(ANY), spec(VMEM)],
        scratch_shapes=[
            VMEM((8, 16, 2, 8, WIDTH), BF16),
            VMEM((512, 2, 8, WIDTH), BF16),
            VMEM((512, 3, 2, 8, HARM), F32),
            VMEM((8, 2, 128), jnp.int32),
            SMEM((8, 2, 128), jnp.int32),
            VMEM((256, EXT), F32),
            VMEM((256, 128), F32),
            VMEM((512, 128), F32),
            VMEM((8, ANG, 256), F32),
            VMEM((8, ANG, 256), F32),
            VMEM((ANG, 256), F32),
            VMEM((128, EXT), BF16),
            DMA((5,)), DMA((112,)), DMA((112,)),
        ],
        compiler_params=pltpu.CompilerParams(
            collective_id=0, has_side_effects=True, vmem_limit_bytes=48 * 2**20
        ),
    )(
        particles.reshape(count, 8, 2, 8, WIDTH),
        references.reshape(groups, 8, 2, 8, WIDTH),
        own_cand,
        fwd,
    )
    sums, own, totals = pl.pallas_call(
        sums_kernel,
        out_shape=(
            sds((512, 8, WIDTH), BF16),
            sds((2, 4, 16, 8, WIDTH), F32),
            sds((8, 128), F32),
        ),
        in_specs=[spec(SMEM), spec(ANY), spec(ANY), spec(ANY)],
        out_specs=[spec(ANY), spec(ANY), spec(VMEM)],
        scratch_shapes=[
            VMEM((256, 8, WIDTH), BF16),
            VMEM((2, 8, ANG, 256), F32),
            VMEM((6 * ANG, EXT), BF16),
            VMEM((256, CANDS, WIDTH), F32),
            VMEM((256, CANDS, 128), F32),
            VMEM((512, 8, WIDTH), F32),
            VMEM((512, 128), F32),
            VMEM((512, 8, WIDTH), BF16),
            DMA((3,)), DMA((12,)),
        ],
        compiler_params=pltpu.CompilerParams(vmem_limit_bytes=56 * 2**20),
    )(cand.reshape(32, 128), halves.reshape(256, 8, WIDTH), weights, bwd)
    class_sums, class_tot = pl.pallas_call(
        scatter_kernel,
        out_shape=(sds((16, 2, 8, WIDTH), F32), sds((8, 128), F32)),
        in_specs=[spec(ANY), spec(ANY), spec(VMEM)],
        out_specs=[spec(VMEM), spec(VMEM)],
        scratch_shapes=[VMEM((2, 2, 4, 8, 8, WIDTH), BF16)] * 5
        + [
            VMEM((2, 4, 16, 8, WIDTH), F32),
            VMEM((2, 4, 16, 8, WIDTH), BF16),
            VMEM((2, 4, 16, 8, WIDTH), BF16),
            VMEM((2, 16, 8, WIDTH), F32),
            VMEM((16, 8, 128), F32),
            DMA((6,)), DMA((41,)), DMA((41,)), DMA((16,)), DMA((16,)),
        ],
        compiler_params=pltpu.CompilerParams(
            collective_id=1, has_side_effects=True, vmem_limit_bytes=48 * 2**20
        ),
    )(sums.reshape(4, 4, 2, 2, 8, 8, WIDTH), own, totals)
    row = lax.dynamic_index_in_dim(class_tot, lax.axis_index("cls") // 8, 0, keepdims=False)
    class_weights = lax.dynamic_slice_in_dim(row, place, 16)
    log_norm = lse[0].reshape(count, CANDS)[:, 0]
    return (class_sums.reshape(groups, 16, WIDTH), class_weights, log_norm)


def solution(mesh):
    in_specs = (
        P(("cls", "prt"), None, None),
        P("cls", None, None),
        P(("cls", "prt"), None),
        P(("cls", "prt"), None, None),
    )
    out_specs = (P("cls", "prt", None), P("cls"), P(("cls", "prt")))
    return jax.shard_map(
        per_device, mesh=mesh, in_specs=in_specs, out_specs=out_specs, check_vma=False
    )
```

time: 204 us -> 149 us (0.73)
  Pallas kernels: 191 us -> 137 us
    pallas_call x1, Pallas kernels: 64.2 us -> 26.9 us  [per_device(): pl.pallas_call(sums_kernel, out_shape=(sds((512, 8, WIDTH), BF16), sds((2...]
    pallas_call x1, Pallas kernels: 88.5 us -> 76.8 us  [per_device(): pl.pallas_call(assign_kernel, out_shape=(sds((2, 8, 16, 8, WIDTH), BF16),...]
    pallas_call x1, Pallas kernels: 38.7 us -> 32.8 us  [per_device(): pl.pallas_call(scatter_kernel, out_shape=(sds((16, 2, 8, WIDTH), F32), sd...]
where the time goes in v3:
time: 149 us
  Pallas kernels  137 us (92%)
  local copies, waits for them, and re-layouts  9.84 us (7%)
  other arithmetic  1.52 us (1%)
    pallas_call x1, Pallas kernels, per_device(): pl.pallas_call(assign_kernel, out_shape=(sds((2, 8, 16, 8, WIDTH), BF16),...  76.8 us
    pallas_call x1, Pallas kernels, per_device(): pl.pallas_call(scatter_kernel, out_shape=(sds((16, 2, 8, WIDTH), F32), sd...  32.8 us
    pallas_call x1, Pallas kernels, per_device(): pl.pallas_call(sums_kernel, out_shape=(sds((512, 8, WIDTH), BF16), sds((2...  26.9 us
    unnamed x16, local copies, waits for them, and re-layouts  8.96 us

profile of v3, /device:TPU:1, one launch (start us, length us, event | category | flops | bytes accessed | tf_op | source)
XLA Modules:
  0.0 148.7 jit_solution(9866529604971323377)
XLA Ops:
  0.7 0.7 broadcast_multiply_fusion
  1.4 0.1 copy.11
  1.5 0.8 slice_add_fusion
  2.3 0.1 reshape.32.cand
  2.4 0.0 copy-start
  2.4 1.6 %copy-done = bf16[16,128,512]{2,1,0:T(8,128)(2,1)S(1)} copy-done((bf16[16,128,512]{2,1,0:T(8,128)(2,1)S(1)}, bf16[16,128,512]{2,1,0:T(8,128)(2,1)}, u32[]{:S(2)}) %copy-start) | copy-done | bytes 2097176
  4.0 0.0 copy-start.4
  4.0 0.9 copy-done.4
  4.9 76.8 %shard_map.85 = (bf16[2,8,16,8,512]{4,3,2,1,0:T(8,128)(2,1)S(1)}, f32[2,8,40,256]{3,2,1,0:T(8,128)S(1)}, s32[2,8,2,128]{3,2,1,0:T(2,128)S(1)}, f32[8,256]{1,0:T(8,128)S(1)}) custom-call(bf16[16,8,2,8,512]{4,3,2,1,0:T(8,128)(2,1)S(1)} %bitcast.10, bf16[16,8,2,8,512]{4,3,2,1,0:T(8,128)(2,1)} %bitcast.15, s32[2,128]{1,0:T(2,128)S(1)} %reshape.32.cand, ...), custom_call_target="tpu_custom_call" | custom-call | tf_op jit(solution)/shard_map/pallas_call | solution.py:553
  81.8 0.0 copy-start.1
  81.8 1.3 copy-done.1
  83.1 0.0 copy-start.3
  83.1 0.9 copy-done.3
  84.0 0.0 copy-start.5
  84.0 0.6 copy-done.5
  84.6 0.1 reshape_squeeze.3
  84.7 0.6 copy.13
  85.3 26.9 %shard_map.86 = (bf16[512,8,512]{2,1,0:T(8,128)(2,1)}, f32[2,4,16,8,512]{4,3,2,1,0:T(8,128)}, f32[8,128]{1,0:T(8,128)}) custom-call(s32[32,128]{1,0:T(8,128)} %bitcast.13, bf16[256,8,512]{2,1,0:T(8,128)(2,1)} %bitcast.11, f32[2,8,40,256]{3,2,1,0:T(8,128)} %copy-done.3, bf16[240,640]{1,0:T(8,128)(2,1)} %constant.78.clone.bwd_hbm), custom_call_target="tpu_custom_call" | custom-call | tf_op jit(solution)/shard_map/pallas_call | solution.py:587
  112.2 0.0 copy-start.2
  112.2 1.6 %copy-done.2 = f32[2,4,16,8,512]{4,3,2,1,0:T(8,128)S(1)} copy-done((f32[2,4,16,8,512]{4,3,2,1,0:T(8,128)S(1)}, f32[2,4,16,8,512]{4,3,2,1,0:T(8,128)}, u32[]{:S(2)}) %copy-start.2) | copy-done | bytes 2097176
  113.8 0.7 copy-done.6
  114.4 32.8 %shard_map.87 = (f32[16,2,8,512]{3,2,1,0:T(8,128)S(1)}, f32[8,128]{1,0:T(8,128)S(1)}) custom-call(bf16[4,4,2,2,8,8,512]{6,5,4,3,2,1,0:T(8,128)(2,1)} %bitcast.14, f32[2,4,16,8,512]{4,3,2,1,0:T(8,128)S(1)} %copy-done.2, f32[8,128]{1,0:T(8,128)S(1)} %copy-done.6), custom_call_target="tpu_custom_call" | custom-call | tf_op jit(solution)/shard_map/pallas_call | solution.py:609
  147.3 0.6 dynamic-slice_bitcast_fusion
  147.9 0.8 copy.15
  (2 shorter events, 0.0 us)
Async XLA Ops:
  2.4 1.6 %copy-start = (bf16[16,128,512]{2,1,0:T(8,128)(2,1)S(1)}, bf16[16,128,512]{2,1,0:T(8,128)(2,1)}, u32[]{:S(2)}) copy-start(bf16[16,128,512]{2,1,0:T(8,128)(2,1)} %param.6) | copy-start | bytes 6291460
  4.0 0.9 copy-start.4
  81.8 1.3 copy-start.1
  83.1 0.9 copy-start.3
  84.0 0.6 copy-start.5
  112.2 1.6 %copy-start.2 = (f32[2,4,16,8,512]{4,3,2,1,0:T(8,128)S(1)}, f32[2,4,16,8,512]{4,3,2,1,0:T(8,128)}, u32[]{:S(2)}) copy-start(f32[2,4,16,8,512]{4,3,2,1,0:T(8,128)} %get-tuple-element.16.own_hbm) | copy-start | bytes 6291460
  113.8 0.7 copy-start.6

commit v4 on v3

--- a/solution.py
+++ b/solution.py
@@ -18,7 +18,7 @@
 CANDS = OWN_TOP * CAND_OWN
 ANG = 40
 EXT = WIDTH + 128
-VMEM, SMEM, ANY = pltpu.VMEM, pltpu.SMEM, pl.ANY
+VMEM, SMEM, HBM = pltpu.VMEM, pltpu.SMEM, pltpu.HBM
 F32, BF16 = jnp.float32, jnp.bfloat16
 DMA = pltpu.SemaphoreType.DMA
 SCALE = 2.0 / math.sqrt(CYCLES * WIDTH)
@@ -147,8 +147,10 @@
     for k, dx, dy in ((16, 1, 0), (17, -1, 0), (18, 0, 1), (19, 0, -1)):
         send(own_refs, piece(me), k, go(dx, dy), z)
     send(own_refs, piece(me), 64, mate, z)
-    for d in around:
-        send(part.at[:, (z + d) % 8], pbuf.at[z], 80 + d, me, (z + d) % 8)
+    for h in range(2):
+        for d in around:
+            rows = pl.ds(8 * h, 8)
+            send(part.at[rows, (z + d) % 8], pbuf.at[z, rows], 80 + 32 * h + d, me, (z + d) % 8)
     own = [
         pltpu.make_async_copy(cand, cbuf.at[z], lsem.at[0]),
         pltpu.make_async_copy(own_refs, piece(me), lsem.at[1]),
@@ -246,98 +248,105 @@
     scp.wait()
     fwd_cp.wait()
 
-    @pl.loop(0, 8)
-    def _(t):
-        d = (t % 2) * ((t + 1) // 2) + (1 - t % 2) * ((8 - t // 2) % 8)
-        src = (z - d + 8) % 8
-
-        @pl.when(t > 0)
-        def _():
-            arrive(pbuf.at[src], 80 + d)
-
-        @pl.loop(0, 2)
-        def _(hi):
+    angle = lax.broadcasted_iota(jnp.int32, (ANG, 128), 0)
+
+    def score(h, first, last):
+        @pl.loop(first, last)
+        def _(t):
+            d = (t % 2) * ((t + 1) // 2) + (1 - t % 2) * ((8 - t // 2) % 8)
+            src = (z - d + 8) % 8
+
+            @pl.when(t > 0)
+            def _():
+                arrive(pbuf.at[src, pl.ds(8 * h, 8)], 80 + 32 * h + d)
+
             @pl.loop(0, 8)
             def _(lo):
-                i = hi * 8 + lo
-                p = pbuf[src, i].astype(F32)
+                p = pbuf[src, h * 8 + lo].astype(F32)
                 p_re, p_im = p[:, :, :HARM], p[:, :, HARM:]
                 p_sum = p_re + p_im
                 for j0 in (0, 8):
                     re, im = [], []
-                    row = pl.multiple_of(i * CANDS + j0, 8)
+                    row = pl.multiple_of(lo * CANDS + j0, 8)
                     for j in range(8):
-                        c = csm[src, hi, lo * CANDS + (j0 + j)]
+                        c = csm[src, h, lo * CANDS + (j0 + j)]
                         k1 = jnp.sum(p_sum * rcomb[c, 0], axis=0)
                         k2 = jnp.sum(p_re * rcomb[c, 1], axis=0)
                         k3 = jnp.sum(p_im * rcomb[c, 2], axis=0)
                         re.append(k1 + k3)
                         im.append(k1 - k2)
-                        normrow[pl.ds(i * CANDS + j0 + j, 1), :] = norms[pl.ds(c, 1), :]
+                        normrow[pl.ds(lo * CANDS + j0 + j, 1), :] = norms[pl.ds(c, 1), :]
                     cross[pl.ds(row, 8), :HARM] = row_sums(re)
                     cross[pl.ds(row, 8), HARM:WIDTH] = row_sums(im)
 
-        cross[:, WIDTH:] = normrow[...]
-        total = jnp.zeros((ANG, 256), F32)
-        for part3 in parts3(cross[...]):
-            out = lax.dot_general(
-                fwd[...], part3, (((1,), (1,)), ((), ())), preferred_element_type=F32
-            )
-            total = total + (out[:ANG] + (out[ANG : 2 * ANG] + out[2 * ANG : 3 * ANG]))
-        cout[d] = total
-
-        @pl.when(t > 0)
-        def _():
-            remote(cout.at[d], cin.at[d], ssem.at[88 + d], rsem.at[88 + d], me, src).start()
-
+            cross[:, WIDTH:] = normrow[...]
+            total = jnp.zeros((ANG, 128), F32)
+            for part3 in parts3(cross[...]):
+                out = lax.dot_general(
+                    fwd[...], part3, (((1,), (1,)), ((), ())), preferred_element_type=F32
+                )
+                total = total + (out[:ANG] + (out[ANG : 2 * ANG] + out[2 * ANG : 3 * ANG]))
+            cout[h, d] = total
+
+            @pl.when(t > 0)
+            def _():
+                k = 88 + 32 * h + d
+                remote(cout.at[h, d], cin.at[h, d], ssem.at[k], rsem.at[k], me, src).start()
+
+    def weigh(h):
+        corr = cout[h, 0]
+        for d in range(1, 8):
+            arrive(cin.at[h, d], 88 + 32 * h + d)
+            corr = corr + cin[h, d]
+        score_h = jnp.where(angle < ROTS, corr * SCALE, -1e30)
+        top = group_all(jnp.broadcast_to(jnp.max(score_h, axis=0, keepdims=True), (8, 128)), jnp.maximum)
+        expo = jnp.where(angle < ROTS, jnp.exp(score_h - top[:1]), 0.0)
+        den = group_all(jnp.broadcast_to(jnp.sum(expo, axis=0, keepdims=True), (8, 128)), jnp.add)
+        lse = top + jnp.log(den)
+        lse_out[:, 128 * h : 128 * h + 128] = lse
+        wown[h] = jnp.where(angle < ROTS, jnp.exp(score_h - lse[:1]), 0.0)
+        for d in around:
+            send(wown.at[h], weights.at[core, z, h], 96 + 32 * h + d, me, (z + d) % 8)
+        send(wown.at[h], weights.at[core, z, h], 104 + 32 * h, mate, z)
+
+    score(0, 0, 8)
+    score(1, 0, 8)
+    weigh(0)
     halves_cp = pltpu.make_async_copy(pbuf.at[:, :, core], halves.at[core], lsem.at[2])
     halves_cp.start()
     send(pbuf.at[:, :, 1 - core], halves.at[core], 13, mate, z)
-    corr = cout[0]
-    for d in range(1, 8):
-        arrive(cin.at[d], 88 + d)
-        corr = corr + cin[d]
-    angle = lax.broadcasted_iota(jnp.int32, (ANG, 128), 0)
-    for lanes in (slice(0, 128), slice(128, 256)):
-        score = jnp.where(angle < ROTS, corr[:, lanes] * SCALE, -1e30)
-        top = group_all(jnp.broadcast_to(jnp.max(score, axis=0, keepdims=True), (8, 128)), jnp.maximum)
-        expo = jnp.where(angle < ROTS, jnp.exp(score - top[:1]), 0.0)
-        den = group_all(jnp.broadcast_to(jnp.sum(expo, axis=0, keepdims=True), (8, 128)), jnp.add)
-        lse = top + jnp.log(den)
-        lse_out[:, lanes] = lse
-        wown[:, lanes] = jnp.where(angle < ROTS, jnp.exp(score - lse[:1]), 0.0)
-    for d in around:
-        send(wown, weights.at[core, z], 96 + d, me, (z + d) % 8)
-    send(wown, weights.at[core, z], 104, mate, z)
+    weigh(1)
     w_own = pltpu.make_async_copy(wown, weights.at[core, z], lsem.at[1])
     w_own.start()
-    for d in (1, 7, 2, 6, 3, 5, 4):
-        land = weights.at[core, (z - d + 8) % 8]
-        arrive(land, 96 + d)
-        pass_on(land, 104 + d, mate)
-
-    for d in range(8):
-        arrive(weights.at[1 - core, (z - d + 8) % 8], 104 + d)
+    for h in range(2):
+        for d in around:
+            land = weights.at[core, (z - d + 8) % 8, h]
+            arrive(land, 96 + 32 * h + d)
+            pass_on(land, 104 + 32 * h + d, mate)
+
+    for h in range(2):
+        for d in range(8):
+            arrive(weights.at[1 - core, (z - d + 8) % 8, h], 104 + 32 * h + d)
     arrive(cand_out.at[1 - core], 12)
     arrive(halves.at[1 - core], 13)
     for cp in (w_own, c_back, halves_cp):
         cp.wait()
     for cp in sent:
         cp.wait_send()
-    for d in range(1, 8):
-        remote(cout.at[d], cin.at[d], ssem.at[88 + d], rsem.at[88 + d], me, z).wait_send()
+    for h in range(2):
+        for d in range(1, 8):
+            k = 88 + 32 * h + d
+            remote(cout.at[h, d], cin.at[h, d], ssem.at[k], rsem.at[k], me, z).wait_send()
 
 
 def sums_kernel(
-    cand, halves_hbm, w_hbm, bwd_hbm,
-    out_ref, own_ref, tot_ref,
-    halves, w_ref, bwd, mixed, tots, acc, accw, obuf, lsem, osem,
+    cand_in, halves, w_ref, bwd_hbm,
+    out_ref, acc, tot_ref,
+    cand, bwd, mixed, tots, accw, lsem,
 ):
-    x, y, _, _ = where_am_i()
     loads = [
-        pltpu.make_async_copy(w_hbm, w_ref, lsem.at[0]),
-        pltpu.make_async_copy(bwd_hbm, bwd, lsem.at[1]),
-        pltpu.make_async_copy(halves_hbm, halves, lsem.at[2]),
+        pltpu.make_async_copy(bwd_hbm, bwd, lsem.at[0]),
+        pltpu.make_async_copy(cand_in, cand, lsem.at[1]),
     ]
     for cp in loads:
         cp.start()
@@ -347,12 +356,12 @@
         acc[pl.ds(c * 8, 8)] = jnp.zeros((8, 8, WIDTH), F32)
 
     accw[...] = jnp.zeros_like(accw)
-    loads[0].wait()
-    loads[1].wait()
+    for cp in loads:
+        cp.wait()
 
     @pl.loop(0, 16)
     def _(b):
-        w = w_ref[b // 8, b % 8]
+        w = jnp.concatenate([w_ref[b // 8, b % 8, 0], w_ref[b // 8, b % 8, 1]], 1)
         high, mid, low = [v.astype(F32) for v in parts3(w)]
         lhs = jnp.concatenate([high, mid, low, high, mid, high], 0).astype(BF16)
         y = lax.dot_general(
@@ -361,8 +370,6 @@
         block = pl.ds(b * 16, 16)
         mixed[block] = y[:, :WIDTH].astype(BF16).astype(F32).reshape(16, CANDS, WIDTH)
         tots[block] = y[:, WIDTH:].reshape(16, CANDS, 128)
-
-    loads[2].wait()
 
     @pl.loop(0, 32)
     def _(b):
@@ -389,22 +396,10 @@
                     acc[c, :, HARM:] = im
                     accw[pl.ds(c, 1), :] = tot
 
-    out = []
-    for k in range(4):
-        out.append(pltpu.make_async_copy(acc.at[pl.ds((x * 8 + k * 2) * 16, 16)], own_ref.at[0, k], osem.at[k]))
-        out.append(pltpu.make_async_copy(acc.at[pl.ds((k * 8 + y * 2 + 1) * 16, 16)], own_ref.at[1, k], osem.at[4 + k]))
-    for cp in out:
-        cp.start()
-    for k in range(4):
-
-        @pl.loop(0, 16)
-        def _(c, k=k):
-            at = pl.ds(k * 128 + c * 8, 8)
-            obuf[at] = acc[at].astype(BF16)
-
-        at = pl.ds(k * 128, 128)
-        out.append(pltpu.make_async_copy(obuf.at[at], out_ref.at[at], osem.at[8 + k]))
-        out[-1].start()
+    @pl.loop(0, 64)
+    def _(c):
+        out_ref[pl.ds(c * 8, 8)] = acc[pl.ds(c * 8, 8)].astype(BF16)
+
     diag = lax.broadcasted_iota(jnp.int32, (128, 128), 0) == lax.broadcasted_iota(
         jnp.int32, (128, 128), 1
     )
@@ -413,14 +408,12 @@
         for b in range(4)
     ]
     tot_ref[...] = jnp.concatenate(rows + [jnp.zeros((4, 128), F32)], 0)
-    for cp in out:
-        cp.wait()
 
 
 def scatter_kernel(
-    part, own_hbm, tot,
+    part, own, tot,
     out_ref, tot_out,
-    relay, direct, joined, mine, send3, own32, s2, r2, fin, totin,
+    relay, direct, joined, send3, s2, r2, fin, totin,
     lsem, ssem, rsem, tsend, trecv,
 ):
     x, y, core, z = where_am_i()
@@ -459,29 +452,24 @@
         u = (x, y)[k]
         send(sel(k, u + 1, 1), direct.at[k, 0], 8 * k + 2, step(k, 1, True))
         send(sel(k, u - 1, 0), direct.at[k, 1], 8 * k + 3, step(k, -1, True))
-    loads = []
-    for k in range(2):
-        u = (x, y)[k]
-        loads.append(pltpu.make_async_copy(sel(k, u + 1, 0), mine.at[k, 0], lsem.at[3 * k]))
-        loads.append(pltpu.make_async_copy(sel(k, u - 1, 1), mine.at[k, 1], lsem.at[3 * k + 1]))
-        loads.append(pltpu.make_async_copy(own_hbm.at[k], own32.at[k], lsem.at[3 * k + 2]))
-    for cp in loads:
-        cp.start()
-    for cp in loads:
-        cp.wait()
+    def partial(k, to, w, q):
+        g = (to % 4) * 8 + w * 2 if k == 0 else w * 8 + (to % 4) * 2 + 1
+        return own[g * 16 + q]
+
     rounds = (2, 1, 3, 0)
     for k in range(2):
-        v = (y, x)[k]
+        u, v = (x, y)[k], (y, x)[k]
         for side in range(2):
             arrive(relay.at[k, side], 8 * k + side)
         for e in rounds:
             w = (v + e) % 4
             for side in range(2):
+                to = u + 1 + 2 * side
 
                 @pl.loop(0, 8)
-                def _(q, k=k, w=w, side=side):
+                def _(q, k=k, w=w, side=side, to=to):
                     send3[k, side, w, q] = (
-                        relay[k, side, w, q].astype(F32) + mine[k, side, w, q].astype(F32)
+                        relay[k, side, w, q].astype(F32) + partial(k, to, w, side * 8 + q)
                     ).astype(BF16)
 
                 n = 16 + 8 * k + 2 * e + side
@@ -491,15 +479,15 @@
             arrive(direct.at[k, side], 8 * k + 2 + side)
     for e in rounds:
         for k in range(2):
-            v = (y, x)[k]
+            u, v = (x, y)[k], (y, x)[k]
             w = (v + e) % 4
             for side in range(2):
                 arrive(joined.at[k, side, w], 16 + 8 * k + 2 * e + side)
 
             @pl.loop(0, 8)
-            def _(q, k=k, w=w, e=e):
+            def _(q, k=k, u=u, w=w, e=e):
                 for side in range(2):
-                    total = own32[k, w, side * 8 + q] + (
+                    total = partial(k, u, w, side * 8 + q) + (
                         joined[k, side, w, q].astype(F32) + direct[k, 1 - side, w, q].astype(F32)
                     )
                     if e:
@@ -554,29 +542,29 @@
         assign_kernel,
         out_shape=(
             sds((2, 8, 16, 8, WIDTH), BF16),
-            sds((2, 8, ANG, 256), F32),
+            sds((2, 8, 2, ANG, 128), F32),
             sds((2, 8, 2, 128), jnp.int32),
             sds((8, 256), F32),
         ),
-        in_specs=[spec(ANY), spec(ANY), spec(VMEM), spec(ANY)],
-        out_specs=[spec(ANY), spec(ANY), spec(ANY), spec(VMEM)],
+        in_specs=[spec(HBM), spec(HBM), spec(VMEM), spec(HBM)],
+        out_specs=[spec(VMEM)] * 4,
         scratch_shapes=[
             VMEM((8, 16, 2, 8, WIDTH), BF16),
             VMEM((512, 2, 8, WIDTH), BF16),
             VMEM((512, 3, 2, 8, HARM), F32),
             VMEM((8, 2, 128), jnp.int32),
             SMEM((8, 2, 128), jnp.int32),
-            VMEM((256, EXT), F32),
-            VMEM((256, 128), F32),
+            VMEM((128, EXT), F32),
+            VMEM((128, 128), F32),
             VMEM((512, 128), F32),
-            VMEM((8, ANG, 256), F32),
-            VMEM((8, ANG, 256), F32),
-            VMEM((ANG, 256), F32),
+            VMEM((2, 8, ANG, 128), F32),
+            VMEM((2, 8, ANG, 128), F32),
+            VMEM((2, ANG, 128), F32),
             VMEM((128, EXT), BF16),
-            DMA((5,)), DMA((112,)), DMA((112,)),
+            DMA((5,)), DMA((144,)), DMA((144,)),
         ],
         compiler_params=pltpu.CompilerParams(
-            collective_id=0, has_side_effects=True, vmem_limit_bytes=48 * 2**20
+            collective_id=0, has_side_effects=True, vmem_limit_bytes=50 * 2**20
         ),
     )(
         particles.reshape(count, 8, 2, 8, WIDTH),
@@ -588,40 +576,36 @@
         sums_kernel,
         out_shape=(
             sds((512, 8, WIDTH), BF16),
-            sds((2, 4, 16, 8, WIDTH), F32),
+            sds((512, 8, WIDTH), F32),
             sds((8, 128), F32),
         ),
-        in_specs=[spec(SMEM), spec(ANY), spec(ANY), spec(ANY)],
-        out_specs=[spec(ANY), spec(ANY), spec(VMEM)],
+        in_specs=[spec(VMEM), spec(VMEM), spec(VMEM), spec(HBM)],
+        out_specs=[spec(VMEM)] * 3,
         scratch_shapes=[
-            VMEM((256, 8, WIDTH), BF16),
-            VMEM((2, 8, ANG, 256), F32),
+            SMEM((32, 128), jnp.int32),
             VMEM((6 * ANG, EXT), BF16),
             VMEM((256, CANDS, WIDTH), F32),
             VMEM((256, CANDS, 128), F32),
-            VMEM((512, 8, WIDTH), F32),
             VMEM((512, 128), F32),
-            VMEM((512, 8, WIDTH), BF16),
-            DMA((3,)), DMA((12,)),
+            DMA((2,)),
         ],
-        compiler_params=pltpu.CompilerParams(vmem_limit_bytes=56 * 2**20),
+        compiler_params=pltpu.CompilerParams(vmem_limit_bytes=20 * 2**20),
     )(cand.reshape(32, 128), halves.reshape(256, 8, WIDTH), weights, bwd)
     class_sums, class_tot = pl.pallas_call(
         scatter_kernel,
         out_shape=(sds((16, 2, 8, WIDTH), F32), sds((8, 128), F32)),
-        in_specs=[spec(ANY), spec(ANY), spec(VMEM)],
+        in_specs=[spec(VMEM)] * 3,
         out_specs=[spec(VMEM), spec(VMEM)],
-        scratch_shapes=[VMEM((2, 2, 4, 8, 8, WIDTH), BF16)] * 5
+        scratch_shapes=[VMEM((2, 2, 4, 8, 8, WIDTH), BF16)] * 4
         + [
-            VMEM((2, 4, 16, 8, WIDTH), F32),
             VMEM((2, 4, 16, 8, WIDTH), BF16),
             VMEM((2, 4, 16, 8, WIDTH), BF16),
             VMEM((2, 16, 8, WIDTH), F32),
             VMEM((16, 8, 128), F32),
-            DMA((6,)), DMA((41,)), DMA((41,)), DMA((16,)), DMA((16,)),
+            DMA((1,)), DMA((41,)), DMA((41,)), DMA((16,)), DMA((16,)),
         ],
         compiler_params=pltpu.CompilerParams(
-            collective_id=1, has_side_effects=True, vmem_limit_bytes=48 * 2**20
+            collective_id=1, has_side_effects=True, vmem_limit_bytes=20 * 2**20
         ),
     )(sums.reshape(4, 4, 2, 2, 8, 8, WIDTH), own, totals)
     row = lax.dynamic_index_in_dim(class_tot, lax.axis_index("cls") // 8, 0, keepdims=False)

time: 149 us -> 139 us (0.933)
  local copies, waits for them, and re-layouts: 9.84 us -> 3.19 us
  Pallas kernels: 137 us -> 133 us
    unnamed x16 -> x6, local copies, waits for them, and re-layouts: 8.96 us -> 2.3 us
    pallas_call x1, Pallas kernels: 26.9 us -> 23.6 us  [per_device(): pl.pallas_call(sums_kernel, out_shape=(sds((512, 8, WIDTH), BF16), sds((5...]
    pallas_call x1, Pallas kernels: 76.8 us -> 75.2 us  [per_device(): pl.pallas_call(assign_kernel, out_shape=(sds((2, 8, 16, 8, WIDTH), BF16),...]
where the time goes in v4:
time: 139 us
  Pallas kernels  133 us (96%)
  local copies, waits for them, and re-layouts  3.19 us (2%)
  other arithmetic  1.52 us (1%)
    pallas_call x1, Pallas kernels, per_device(): pl.pallas_call(assign_kernel, out_shape=(sds((2, 8, 16, 8, WIDTH), BF16),...  75.2 us
    pallas_call x1, Pallas kernels, per_device(): pl.pallas_call(scatter_kernel, out_shape=(sds((16, 2, 8, WIDTH), F32), sd...  34.3 us
    pallas_call x1, Pallas kernels, per_device(): pl.pallas_call(sums_kernel, out_shape=(sds((512, 8, WIDTH), BF16), sds((5...  23.6 us

profile of v4, /device:TPU:1, one launch (start us, length us, event | category | flops | bytes accessed | tf_op | source)
XLA Modules:
  0.0 138.6 jit_solution(14284195979387828541)
XLA Ops:
  0.7 0.7 broadcast_multiply_fusion
  1.4 0.1 copy.11
  1.5 0.8 slice_add_fusion
  2.3 0.1 reshape.32.cand
  2.4 0.0 copy-start.1
  2.4 0.9 copy-done.1
  3.3 0.0 copy-start
  3.3 75.2 %shard_map.85 = (bf16[2,8,16,8,512]{4,3,2,1,0:T(8,128)(2,1)S(1)}, f32[2,8,2,40,128]{4,3,2,1,0:T(8,128)S(1)}, s32[2,8,2,128]{3,2,1,0:T(2,128)S(1)}, f32[8,256]{1,0:T(8,128)S(1)}) custom-call(bf16[16,8,2,8,512]{4,3,2,1,0:T(8,128)(2,1)} %bitcast.14, bf16[16,8,2,8,512]{4,3,2,1,0:T(8,128)(2,1)} %bitcast.15, s32[2,128]{1,0:T(2,128)S(1)} %reshape.32.cand, ...), custom_call_target="tpu_custom_call" | custom-call | tf_op jit(solution)/shard_map/pallas_call | solution.py:541
  78.6 0.1 reshape_squeeze.3
  78.7 0.6 copy.13
  79.3 0.0 copy-done
  79.3 23.6 %shard_map.86 = (bf16[512,8,512]{2,1,0:T(8,128)(2,1)S(1)}, f32[512,8,512]{2,1,0:T(8,128)S(1)}, f32[8,128]{1,0:T(8,128)S(1)}) custom-call(s32[32,128]{1,0:T(8,128)S(1)} %bitcast.13, bf16[256,8,512]{2,1,0:T(8,128)(2,1)S(1)} %bitcast.11, f32[2,8,2,40,128]{4,3,2,1,0:T(8,128)S(1)} %get-tuple-element.14.w_ref, bf16[240,640]{1,0:T(8,128)(2,1)S(1)} %copy-done), custom_call_target="tpu_custom_call" | custom-call | tf_op jit(solution)/shard_map/pallas_call | solution.py:575
  102.9 34.3 %shard_map.87 = (f32[16,2,8,512]{3,2,1,0:T(8,128)S(1)}, f32[8,128]{1,0:T(8,128)S(1)}) custom-call(bf16[4,4,2,2,8,8,512]{6,5,4,3,2,1,0:T(8,128)(2,1)S(1)} %bitcast.10, f32[512,8,512]{2,1,0:T(8,128)S(1)} %get-tuple-element.16.own, f32[8,128]{1,0:T(8,128)S(1)} %get-tuple-element.17.tot), custom_call_target="tpu_custom_call" | custom-call | tf_op jit(solution)/shard_map/pallas_call | solution.py:594
  137.3 0.6 dynamic-slice_bitcast_fusion
  137.8 0.8 copy.15
  (1 shorter events, 0.0 us)
Async XLA Ops:
  2.4 0.9 copy-start.1
  3.3 75.9 %copy-start = (bf16[240,640]{1,0:T(8,128)(2,1)S(1)}, bf16[240,640]{1,0:T(8,128)(2,1)}, u32[]{:S(2)}) copy-start(bf16[240,640]{1,0:T(8,128)(2,1)} %constant.78.clone.bwd_hbm) | copy-start | bytes 921604

commit v5 on v4

--- a/solution.py
+++ b/solution.py
@@ -16,6 +16,7 @@
 OWN_TOP = 4
 CAND_OWN = 4
 CANDS = OWN_TOP * CAND_OWN
+GROUP = 4
 ANG = 40
 EXT = WIDTH + 128
 VMEM, SMEM, HBM = pltpu.VMEM, pltpu.SMEM, pltpu.HBM
@@ -249,6 +250,7 @@
     fwd_cp.wait()
 
     angle = lax.broadcasted_iota(jnp.int32, (ANG, 128), 0)
+    used = pl.ds(0, ROTS)
 
     def score(h, first, last):
         @pl.loop(first, last)
@@ -291,12 +293,12 @@
             @pl.when(t > 0)
             def _():
                 k = 88 + 32 * h + d
-                remote(cout.at[h, d], cin.at[h, d], ssem.at[k], rsem.at[k], me, src).start()
+                remote(cout.at[h, d, used], cin.at[h, d, used], ssem.at[k], rsem.at[k], me, src).start()
 
     def weigh(h):
         corr = cout[h, 0]
         for d in range(1, 8):
-            arrive(cin.at[h, d], 88 + 32 * h + d)
+            arrive(cin.at[h, d, used], 88 + 32 * h + d)
             corr = corr + cin[h, d]
         score_h = jnp.where(angle < ROTS, corr * SCALE, -1e30)
         top = group_all(jnp.broadcast_to(jnp.max(score_h, axis=0, keepdims=True), (8, 128)), jnp.maximum)
@@ -306,8 +308,8 @@
         lse_out[:, 128 * h : 128 * h + 128] = lse
         wown[h] = jnp.where(angle < ROTS, jnp.exp(score_h - lse[:1]), 0.0)
         for d in around:
-            send(wown.at[h], weights.at[core, z, h], 96 + 32 * h + d, me, (z + d) % 8)
-        send(wown.at[h], weights.at[core, z, h], 104 + 32 * h, mate, z)
+            send(wown.at[h, used], weights.at[core, z, h, used], 96 + 32 * h + d, me, (z + d) % 8)
+        send(wown.at[h, used], weights.at[core, z, h, used], 104 + 32 * h, mate, z)
 
     score(0, 0, 8)
     score(1, 0, 8)
@@ -320,13 +322,13 @@
     w_own.start()
     for h in range(2):
         for d in around:
-            land = weights.at[core, (z - d + 8) % 8, h]
+            land = weights.at[core, (z - d + 8) % 8, h, used]
             arrive(land, 96 + 32 * h + d)
             pass_on(land, 104 + 32 * h + d, mate)
 
     for h in range(2):
         for d in range(8):
-            arrive(weights.at[1 - core, (z - d + 8) % 8, h], 104 + 32 * h + d)
+            arrive(weights.at[1 - core, (z - d + 8) % 8, h, used], 104 + 32 * h + d)
     arrive(cand_out.at[1 - core], 12)
     arrive(halves.at[1 - core], 13)
     for cp in (w_own, c_back, halves_cp):
@@ -336,7 +338,7 @@
     for h in range(2):
         for d in range(1, 8):
             k = 88 + 32 * h + d
-            remote(cout.at[h, d], cin.at[h, d], ssem.at[k], rsem.at[k], me, z).wait_send()
+            remote(cout.at[h, d, used], cin.at[h, d, used], ssem.at[k], rsem.at[k], me, z).wait_send()
 
 
 def sums_kernel(
@@ -359,17 +361,19 @@
     for cp in loads:
         cp.wait()
 
-    @pl.loop(0, 16)
-    def _(b):
-        w = jnp.concatenate([w_ref[b // 8, b % 8, 0], w_ref[b // 8, b % 8, 1]], 1)
-        high, mid, low = [v.astype(F32) for v in parts3(w)]
-        lhs = jnp.concatenate([high, mid, low, high, mid, high], 0).astype(BF16)
-        y = lax.dot_general(
-            lhs, bwd[...], (((0,), (0,)), ((), ())), preferred_element_type=F32
-        )
-        block = pl.ds(b * 16, 16)
-        mixed[block] = y[:, :WIDTH].astype(BF16).astype(F32).reshape(16, CANDS, WIDTH)
-        tots[block] = y[:, WIDTH:].reshape(16, CANDS, 128)
+    @pl.loop(0, 8)
+    def _(pair):
+        for b in (2 * pair, 2 * pair + 1):
+            w = jnp.concatenate([w_ref[b // 8, b % 8, 0], w_ref[b // 8, b % 8, 1]], 1)
+            w = jnp.where(lax.broadcasted_iota(jnp.int32, w.shape, 0) < ROTS, w, 0.0)
+            high, mid, low = [v.astype(F32) for v in parts3(w)]
+            lhs = jnp.concatenate([high, mid, low, high, mid, high], 0).astype(BF16)
+            y = lax.dot_general(
+                lhs, bwd[...], (((0,), (0,)), ((), ())), preferred_element_type=F32
+            )
+            block = pl.ds(b * 16, 16)
+            mixed[block] = y[:, :WIDTH].astype(BF16).astype(F32).reshape(16, CANDS, WIDTH)
+            tots[block] = y[:, WIDTH:].reshape(16, CANDS, 128)
 
     @pl.loop(0, 32)
     def _(b):
@@ -377,21 +381,31 @@
         def _(lo):
             p = halves[b * 8 + lo].astype(F32)
             p_re, p_im = p[:, :HARM], p[:, HARM:]
-            for j0 in range(0, CANDS, 8):
-                cs, new, neww = [], [], []
-                for j in range(j0, j0 + 8):
+
+            def load(j0):
+                got = []
+                for j in range(j0, j0 + GROUP):
                     c = cand[b, lo * CANDS + j]
-                    row = mixed[b * 8 + lo, pl.ds(j, 1), :]
+                    got.append((c, acc[c, :, :HARM], acc[c, :, HARM:], accw[pl.ds(c, 1), :]))
+                return got
+
+            held = load(0)
+            for j0 in range(0, CANDS, GROUP):
+                new = []
+                for j, (c, a_re, a_im, a_tot) in enumerate(held):
+                    row = mixed[b * 8 + lo, pl.ds(j0 + j, 1), :]
                     y_re, y_im = row[:, :HARM], row[:, HARM:]
-                    cs.append(c)
                     new.append(
                         (
-                            acc[c, :, :HARM] + (p_re * y_re - p_im * y_im),
-                            acc[c, :, HARM:] + (p_re * y_im + p_im * y_re),
+                            c,
+                            a_re + (p_re * y_re - p_im * y_im),
+                            a_im + (p_re * y_im + p_im * y_re),
+                            a_tot + tots[b * 8 + lo, pl.ds(j0 + j, 1), :],
                         )
                     )
-                    neww.append(accw[pl.ds(c, 1), :] + tots[b * 8 + lo, pl.ds(j, 1), :])
-                for c, (re, im), tot in zip(cs, new, neww):
+                if j0 + GROUP < CANDS:
+                    held = load(j0 + GROUP)
+                for c, re, im, tot in new:
                     acc[c, :, :HARM] = re
                     acc[c, :, HARM:] = im
                     accw[pl.ds(c, 1), :] = tot
@@ -570,7 +584,7 @@
         particles.reshape(count, 8, 2, 8, WIDTH),
         references.reshape(groups, 8, 2, 8, WIDTH),
         own_cand,
-        fwd,
+        pltpu.with_memory_space_constraint(fwd, HBM),
     )
     sums, own, totals = pl.pallas_call(
         sums_kernel,

time: 139 us -> 135 us (0.971)
  Pallas kernels: 133 us -> 130 us
    pallas_call x1, Pallas kernels: 23.6 us -> 21.7 us  [per_device(): pl.pallas_call(sums_kernel, out_shape=(sds((512, 8, WIDTH), BF16), sds((5...]
where the time goes in v5:
time: 135 us
  Pallas kernels  130 us (96%)
  local copies, waits for them, and re-layouts  2.28 us (2%)
  other arithmetic  1.52 us (1%)
    pallas_call x1, Pallas kernels, per_device(): pl.pallas_call(assign_kernel, out_shape=(sds((2, 8, 16, 8, WIDTH), BF16),...  75.3 us
    pallas_call x1, Pallas kernels, per_device(): pl.pallas_call(scatter_kernel, out_shape=(sds((16, 2, 8, WIDTH), F32), sd...  33.5 us
    pallas_call x1, Pallas kernels, per_device(): pl.pallas_call(sums_kernel, out_shape=(sds((512, 8, WIDTH), BF16), sds((5...  21.7 us

profile of v5, /device:TPU:1, one launch (start us, length us, event | category | flops | bytes accessed | tf_op | source)
XLA Modules:
  0.0 135.0 jit_solution(12038265515346211021)
XLA Ops:
  0.7 0.7 broadcast_multiply_fusion
  1.4 0.1 copy.11
  1.5 0.8 slice_add_fusion
  2.3 0.1 reshape.32.cand
  2.4 0.0 copy-start
  2.4 75.3 %shard_map.85 = (bf16[2,8,16,8,512]{4,3,2,1,0:T(8,128)(2,1)S(1)}, f32[2,8,2,40,128]{4,3,2,1,0:T(8,128)S(1)}, s32[2,8,2,128]{3,2,1,0:T(2,128)S(1)}, f32[8,256]{1,0:T(8,128)S(1)}) custom-call(bf16[16,8,2,8,512]{4,3,2,1,0:T(8,128)(2,1)} %bitcast.14, bf16[16,8,2,8,512]{4,3,2,1,0:T(8,128)(2,1)} %bitcast.15, s32[2,128]{1,0:T(2,128)S(1)} %reshape.32.cand, ...), custom_call_target="tpu_custom_call" | custom-call | tf_op jit(solution)/shard_map/pallas_call | solution.py:555
  77.7 0.1 reshape_squeeze.3
  77.8 0.6 copy.13
  78.4 0.0 copy-done
  78.4 21.7 %shard_map.86 = (bf16[512,8,512]{2,1,0:T(8,128)(2,1)S(1)}, f32[512,8,512]{2,1,0:T(8,128)S(1)}, f32[8,128]{1,0:T(8,128)S(1)}) custom-call(s32[32,128]{1,0:T(8,128)S(1)} %bitcast.13, bf16[256,8,512]{2,1,0:T(8,128)(2,1)S(1)} %bitcast.11, f32[2,8,2,40,128]{4,3,2,1,0:T(8,128)S(1)} %get-tuple-element.14.w_ref, bf16[240,640]{1,0:T(8,128)(2,1)S(1)} %copy-done), custom_call_target="tpu_custom_call" | custom-call | tf_op jit(solution)/shard_map/pallas_call | solution.py:589
  100.1 33.5 %shard_map.87 = (f32[16,2,8,512]{3,2,1,0:T(8,128)S(1)}, f32[8,128]{1,0:T(8,128)S(1)}) custom-call(bf16[4,4,2,2,8,8,512]{6,5,4,3,2,1,0:T(8,128)(2,1)S(1)} %bitcast.10, f32[512,8,512]{2,1,0:T(8,128)S(1)} %get-tuple-element.16.own, f32[8,128]{1,0:T(8,128)S(1)} %get-tuple-element.17.tot), custom_call_target="tpu_custom_call" | custom-call | tf_op jit(solution)/shard_map/pallas_call | solution.py:608
  133.6 0.6 dynamic-slice_bitcast_fusion
  134.2 0.8 copy.15
  (1 shorter events, 0.0 us)
Async XLA Ops:
  2.4 76.0 %copy-start = (bf16[240,640]{1,0:T(8,128)(2,1)S(1)}, bf16[240,640]{1,0:T(8,128)(2,1)}, u32[]{:S(2)}) copy-start(bf16[240,640]{1,0:T(8,128)(2,1)} %constant.78.clone.bwd_hbm) | copy-start | bytes 921604
